TPU v7x, 32 devices: a whole 2x2x4 slice. The times are simulated.
32 devices in a mesh: seq: 4 (over y, core), head: 8 (over z, x).
Axes of the slice: x: 2, y: 2, z: 4, core: 2. Of those that a mesh axis runs over, the one named last changes fastest.
Arguments:
- query_rows: bfloat16 [4096, 8192], P(('seq', 'head')), may hold values from -6 to 6
- key_rows: bfloat16 [4096, 1024], P(('seq', 'head')), may hold values from -6 to 6
- value_rows: bfloat16 [4096, 1024], P(('seq', 'head')), may hold values from -6 to 6
- grad_out: bfloat16 [8192, 8192], P(('seq', 'head')), may hold values from -6 to 6
- doc_ids: int32 [32], replicated, may hold values from 0 to 7, never falling along the last dimension, each value on 1 to 7 neighbouring positions
- route_table: int32 [4, 4, 4], replicated, may hold values from 0 to 8, as said below
Outputs:
- attn_out: bfloat16 [8192, 8192], P(('seq', 'head'))
- grad_query: bfloat16 [4096, 8192], P(('seq', 'head'))
- grad_key: bfloat16 [4096, 1024], P(('seq', 'head'))
- grad_value: bfloat16 [4096, 1024], P(('seq', 'head'))
Inputs may be any that keep to these rules, and one draw needn't show every extreme that they name: route_table[s, t, c] is a block of sequence shard s (numbered within the shard) that seq index t takes into slot c, or 8 for an empty slot; every block of every shard appears exactly once; live slots come first in each (s, t) row; each shard fills all 4 slots for a quarter of the seq indices, 2 slots for half of them and none for the rest; one seq index has every slot live.
All inputs are finite; a program needn't handle non-finite values.
Results may differ from a plain program's by a relative error of at most 0.015.
Values may be sent and summed in bfloat16 or wider, within the bound.
No kernel may reach another device: no remote copies, remote signals or barrier semaphores. Data moves between devices by JAX's collectives and lax.ppermute only.
A program may use at most 192 MiB of HBM per device.

v0:
```python
import functools
import math

import jax
import jax.numpy as jnp
from jax import lax
from jax.experimental import pallas as pl
from jax.experimental.pallas import tpu as pltpu
from jax.sharding import Mesh
from jax.sharding import PartitionSpec as P


QH = 64
KVH = 8
DH = 128
BLOCK = 128
DOCMAX = 7
HALO = DOCMAX - 1
CHUNKS = 2

ANY = pl.BlockSpec(memory_space=pl.ANY)
NT = (((1,), (1,)), ((), ()))
F32 = jnp.float32
BF16 = jnp.bfloat16


def pack(sources, groups):
    count = sources[0][0].shape[0]
    total = sum(width for _, width, _ in sources)

    def kernel(*refs):
        ins, out_ref, held, sem_in, sem_out = refs[: len(sources)], *refs[len(sources) :]
        loads, stores = [], []
        for r in range(groups):
            at = 0
            for n, (_, width, index) in enumerate(sources):
                col = index(r) * width
                copy = pltpu.make_async_copy(
                    ins[n].at[:, col : col + width],
                    held.at[r, :, at : at + width],
                    sem_in.at[r * len(sources) + n],
                )
                copy.start()
                loads.append(copy)
                at += width
        for r in range(groups):
            for n in range(len(sources)):
                loads[r * len(sources) + n].wait()
            copy = pltpu.make_async_copy(held.at[r], out_ref.at[r], sem_out.at[r])
            copy.start()
            stores.append(copy)
        for copy in stores:
            copy.wait()

    return pl.pallas_call(
        kernel,
        in_specs=[ANY] * len(sources),
        out_specs=ANY,
        out_shape=jax.ShapeDtypeStruct((groups, count, total), BF16),
        scratch_shapes=[
            pltpu.VMEM((groups, count, total), BF16),
            pltpu.SemaphoreType.DMA((groups * len(sources),)),
            pltpu.SemaphoreType.DMA((groups,)),
        ],
        cost_estimate=pl.CostEstimate(
            flops=0, bytes_accessed=4 * groups * count * total, transcendentals=0
        ),
        compiler_params=pltpu.CompilerParams(vmem_limit_bytes=62 << 20),
    )(*[rows for rows, _, _ in sources])


def pack_first(query_rows, key_rows, value_rows, groups):
    width = QH // groups * DH
    repeats = groups // KVH
    sources = [
        (query_rows, width, lambda r: r),
        (key_rows, DH, lambda r: r // repeats),
        (value_rows, DH, lambda r: r // repeats),
    ]
    return pack(sources, groups)


def pack_half(rows, chunk, groups):
    half = QH // groups * DH // CHUNKS
    return pack([(rows, half, lambda r: r * CHUNKS + chunk)], groups)


def relay_in(plane_index, arrived, width):
    n_plane, per_plane = arrived.shape[:2]
    kv = 2 * DH

    def kernel(plane_ref, in_ref, *refs):
        firsts, refs = refs[:n_plane], refs[n_plane:]
        seconds, (one, two, sem_in, sem_out) = refs[:n_plane], refs[n_plane:]
        loads, stores = [], []
        for k in range(n_plane):
            to = plane_ref[0] ^ k
            near = jnp.maximum(to - 1, 0)
            views = [
                (in_ref.at[to, :, :, :width], one.at[k, :, :, :width]),
                (in_ref.at[to, :, :, 2 * width :], one.at[k, :, :, width : width + kv]),
                (in_ref.at[near, :, :, 2 * width :], one.at[k, :, :, width + kv :]),
                (in_ref.at[to, :, :, width : 2 * width], two.at[k]),
            ]
            for n, (src, dst) in enumerate(views):
                copy = pltpu.make_async_copy(src, dst, sem_in.at[4 * k + n])
                copy.start()
                loads.append(copy)
        for k in range(n_plane):
            for copy in loads[4 * k : 4 * k + 4]:
                copy.wait()
            for n, (src, dst) in enumerate(((one.at[k], firsts[k]), (two.at[k], seconds[k]))):
                copy = pltpu.make_async_copy(src, dst, sem_out.at[2 * k + n])
                copy.start()
                stores.append(copy)
        for copy in stores:
            copy.wait()

    one = (per_plane, BLOCK, width + 2 * kv)
    two = (per_plane, BLOCK, width)
    results = pl.pallas_call(
        kernel,
        in_specs=[pl.BlockSpec(memory_space=pltpu.SMEM), ANY],
        out_specs=[ANY] * (2 * n_plane),
        out_shape=[jax.ShapeDtypeStruct(one, BF16)] * n_plane
        + [jax.ShapeDtypeStruct(two, BF16)] * n_plane,
        scratch_shapes=[
            pltpu.VMEM((n_plane, *one), BF16),
            pltpu.VMEM((n_plane, *two), BF16),
            pltpu.SemaphoreType.DMA((4 * n_plane,)),
            pltpu.SemaphoreType.DMA((2 * n_plane,)),
        ],
        cost_estimate=pl.CostEstimate(flops=0, bytes_accessed=6 << 20, transcendentals=0),
        compiler_params=pltpu.CompilerParams(vmem_limit_bytes=62 << 20),
        name="relay_in",
    )(plane_index, arrived)
    return list(results[:n_plane]), list(results[n_plane:])


def relay_out(plane_index, parts, held):
    n_plane = len(parts)
    per_plane, _, width = parts[0].shape
    first_row = held.shape[1] - BLOCK

    def kernel(plane_ref, *refs):
        ins, (_, out_ref, buf, sem_in, sem_out) = refs[:n_plane], refs[n_plane:]
        loads, stores = [], []
        for k in range(n_plane):
            copy = pltpu.make_async_copy(ins[k], buf.at[k], sem_in.at[k])
            copy.start()
            loads.append(copy)
        for k in range(n_plane):
            loads[k].wait()
            at = (plane_ref[0] ^ k) * per_plane
            copy = pltpu.make_async_copy(
                buf.at[k], out_ref.at[pl.ds(at, per_plane), first_row:, :], sem_out.at[k]
            )
            copy.start()
            stores.append(copy)
        for copy in stores:
            copy.wait()

    return pl.pallas_call(
        kernel,
        in_specs=[pl.BlockSpec(memory_space=pltpu.SMEM)] + [ANY] * (n_plane + 1),
        out_specs=ANY,
        out_shape=jax.ShapeDtypeStruct(held.shape, BF16),
        scratch_shapes=[
            pltpu.VMEM((n_plane, per_plane, BLOCK, width), BF16),
            pltpu.SemaphoreType.DMA((n_plane,)),
            pltpu.SemaphoreType.DMA((n_plane,)),
        ],
        input_output_aliases={n_plane + 1: 0},
        cost_estimate=pl.CostEstimate(flops=0, bytes_accessed=2 << 20, transcendentals=0),
        compiler_params=pltpu.CompilerParams(vmem_limit_bytes=62 << 20),
        name="relay_out",
    )(plane_index, *parts, held)


def attend(table, kv_parts, query_parts, grad_slots, carried, last, shard_blocks, out_form):
    n_src = len(kv_parts)
    per_src = kv_parts[0].shape[0]
    blocks = shard_blocks
    width = grad_slots.shape[-1]
    slots = grad_slots.shape[0]
    per_core = slots // out_form[0]
    base = blocks - HALO
    span = blocks + HALO
    pairs = width // (2 * DH)
    scale = 1.0 / math.sqrt(DH)
    exponent = scale * math.log2(math.e)
    first = carried is None

    def kernel(*refs):
        refs = list(refs)
        tab = refs.pop(0)
        kv_refs = [refs.pop(0) for _ in range(n_src)]
        q_refs = kv_refs if first else [refs.pop(0) for _ in range(n_src)]
        go_ref = refs.pop(0)
        carried_ref = None if first else refs.pop(0)
        out_ref = refs.pop(0)
        if last:
            gq_ref, main_ref, back_ref = refs.pop(0), refs.pop(0), refs.pop(0)
        else:
            gq_refs = [refs.pop(0) for _ in range(n_src)]
            acc_out = refs.pop(0)
        qs, gs, kvs, kts, vts, acc, os, gqs, zero, sem_in, sem_go, sem_out, sem_end = refs[:13]
        if last:
            backs = refs[13]
        plane = tab[2 * blocks]
        core = tab[2 * blocks + 1]

        loads = []

        def load(src, dst):
            copy = pltpu.make_async_copy(src, dst, sem_in.at[len(loads)])
            copy.start()
            loads.append(copy)

        for k in range(n_src):
            at = (plane ^ k) * per_src
            load(kv_refs[k].at[:, :, width : width + 2 * DH], kvs.at[pl.ds(blocks + at, per_src)])
            load(kv_refs[k].at[:, :, width + 2 * DH :], kvs.at[pl.ds(at, per_src)])
            load(q_refs[k].at[:, :, :width], qs.at[pl.ds(at, per_src)])
        if not first:
            load(carried_ref, acc)

        def slot_ref(slot):
            row = pl.multiple_of(slot % per_core * BLOCK, BLOCK)
            return out_ref.at[slot // per_core, pl.ds(row, BLOCK), :]

        def go_copy(i):
            return pltpu.make_async_copy(go_ref.at[tab[i]], gs.at[i], sem_go.at[i])

        def out_copy(i):
            return pltpu.make_async_copy(os.at[i], slot_ref(tab[i]), sem_out.at[i])

        @pl.loop(0, blocks)
        def _(i):
            go_copy(i).start()

        zero[...] = jnp.zeros_like(zero)
        for slot in range(slots):
            @pl.when(tab[2 * blocks + 2 + slot] == 0)
            def _():
                pltpu.make_async_copy(zero, slot_ref(slot), sem_end.at[slot]).start()

        if first:
            acc[...] = jnp.zeros_like(acc)
        for copy in loads:
            copy.wait()

        @pl.loop(0, span)
        def _(b):
            at = pl.multiple_of(b * DH, DH)
            kts[:, pl.ds(at, DH)] = kvs[base + b, :, :DH].T
            vts[:, pl.ds(at, DH)] = kvs[base + b, :, DH:].T

        key_at = lax.broadcasted_iota(jnp.int32, (BLOCK, 2 * BLOCK), 0)
        query_at = lax.broadcasted_iota(jnp.int32, (BLOCK, 2 * BLOCK), 1) % BLOCK
        causal = key_at <= query_at

        def block_body(n, i, k):
            start = blocks + i - (n - 1)
            rel = HALO + i - (n - 1)
            size = n * BLOCK
            keys = kvs[pl.ds(start, n), :, :DH].reshape(size, DH)
            values = kvs[pl.ds(start, n), :, DH:].reshape(size, DH)
            lane = pl.multiple_of(rel * DH, DH)
            keys_t = kts[:, pl.ds(lane, size)]
            values_t = vts[:, pl.ds(lane, size)]
            for pair in range(pairs):
                c0 = pair * 2 * DH
                q2 = jnp.concatenate([qs[i, :, c0 : c0 + DH], qs[i, :, c0 + DH : c0 + 2 * DH]], axis=0)
                g2 = jnp.concatenate([gs[i, :, c0 : c0 + DH], gs[i, :, c0 + DH : c0 + 2 * DH]], axis=0)
                s = lax.dot_general(keys, q2, NT, preferred_element_type=F32)
                diag = jnp.where(causal, s[size - BLOCK :], -jnp.inf)
                s = jnp.concatenate([s[: size - BLOCK], diag], axis=0) if n > 1 else diag
                top = jnp.max(s, axis=0, keepdims=True)
                p = jnp.exp2((s - top) * exponent)
                w = p * (1.0 / jnp.sum(p, axis=0, keepdims=True))
                wb = w.astype(BF16)
                o_t = jnp.dot(values_t, wb, preferred_element_type=F32)
                dp = lax.dot_general(values, g2, NT, preferred_element_type=F32)
                delta = jnp.sum(w * dp, axis=0, keepdims=True)
                ds = (w * (dp - delta)).astype(BF16)
                dq_t = jnp.dot(keys_t, ds, preferred_element_type=F32) * scale
                dk = jnp.dot(ds, q2, preferred_element_type=F32)
                dv = jnp.dot(wb, g2, preferred_element_type=F32)
                acc[pl.ds(rel, n), :, :DH] += dk.reshape(n, BLOCK, DH)
                acc[pl.ds(rel, n), :, DH:] += dv.reshape(n, BLOCK, DH)
                for side in range(2):
                    c1 = c0 + side * DH
                    os[i, :, c1 : c1 + DH] = o_t[:, side * BLOCK : (side + 1) * BLOCK].T.astype(BF16)
                    gqs[k, :, c1 : c1 + DH] = dq_t[:, side * BLOCK : (side + 1) * BLOCK].T.astype(BF16)

        @pl.loop(0, blocks)
        def _(k):
            i = core ^ k
            go_copy(i).wait()
            count = tab[blocks + i]
            at = k if last else ((i // per_src) ^ plane) * per_src + i % per_src
            for n in range(1, DOCMAX + 1):
                @pl.when(count == n)
                def _():
                    block_body(n, i, at)
            out_copy(i).start()

        if last:
            @pl.loop(0, HALO)
            def _(b):
                backs[b, :, :DH] = (acc[b, :, :DH] * scale).astype(BF16)
                backs[b, :, DH:] = acc[b, :, DH:].astype(BF16)

        stores = []

        def store(src, dst):
            copy = pltpu.make_async_copy(src, dst, sem_end.at[slots + len(stores)])
            copy.start()
            stores.append(copy)

        if last:
            store(backs, back_ref)
            store(gqs, gq_ref)
            store(acc.at[pl.ds(HALO, blocks)], main_ref)
        else:
            for k in range(n_src):
                store(gqs.at[pl.ds(k * per_src, per_src)], gq_refs[k])
            store(acc, acc_out)

        for copy in stores:
            copy.wait()

        @pl.loop(0, blocks)
        def _(i):
            out_copy(i).wait()

        for slot in range(slots):
            @pl.when(tab[2 * blocks + 2 + slot] == 0)
            def _():
                pltpu.make_async_copy(zero, slot_ref(slot), sem_end.at[slot]).wait()

    operands = [table, *kv_parts]
    if not first:
        operands += query_parts
    operands.append(grad_slots)
    if not first:
        operands.append(carried)
    out_shape = [jax.ShapeDtypeStruct((*out_form, width), BF16)]
    if last:
        out_shape += [
            jax.ShapeDtypeStruct((blocks, BLOCK, width), BF16),
            jax.ShapeDtypeStruct((blocks, BLOCK, 2 * DH), F32),
            jax.ShapeDtypeStruct((HALO, BLOCK, 2 * DH), BF16),
        ]
    else:
        out_shape += [jax.ShapeDtypeStruct((per_src, BLOCK, width), BF16)] * n_src
        out_shape += [jax.ShapeDtypeStruct((span, BLOCK, 2 * DH), F32)]
    scratch = [
        pltpu.VMEM((blocks, BLOCK, width), BF16),
        pltpu.VMEM((blocks, BLOCK, width), BF16),
        pltpu.VMEM((2 * blocks, BLOCK, 2 * DH), BF16),
        pltpu.VMEM((DH, span * BLOCK), BF16),
        pltpu.VMEM((DH, span * BLOCK), BF16),
        pltpu.VMEM((span, BLOCK, 2 * DH), F32),
        pltpu.VMEM((blocks, BLOCK, width), BF16),
        pltpu.VMEM((blocks, BLOCK, width), BF16),
        pltpu.VMEM((BLOCK, width), BF16),
        pltpu.SemaphoreType.DMA((3 * n_src + 1,)),
        pltpu.SemaphoreType.DMA((blocks,)),
        pltpu.SemaphoreType.DMA((blocks,)),
        pltpu.SemaphoreType.DMA((slots + blocks + 3,)),
    ]
    if last:
        scratch.append(pltpu.VMEM((HALO, BLOCK, 2 * DH), BF16))
    work = blocks * width // DH * 4
    results = pl.pallas_call(
        kernel,
        in_specs=[pl.BlockSpec(memory_space=pltpu.SMEM)] + [ANY] * (len(operands) - 1),
        out_specs=[ANY] * len(out_shape),
        out_shape=out_shape,
        scratch_shapes=scratch,
        cost_estimate=pl.CostEstimate(
            flops=work * 10 * BLOCK**3, bytes_accessed=12 << 20, transcendentals=work * BLOCK**2
        ),
        compiler_params=pltpu.CompilerParams(vmem_limit_bytes=62 << 20),
        name="attend_last" if last else "attend_first",
    )(*operands)
    return results


def finish(core_index, rows, main, back):
    blocks, _, width = rows.shape
    base = blocks - HALO
    scale = 1.0 / math.sqrt(DH)

    def kernel(core_ref, rows_ref, main_ref, back_ref, *refs):
        outs, (held, mains, backs, sem_in, sem_out) = refs[:blocks], refs[blocks:]
        core = core_ref[0]
        loads = [
            pltpu.make_async_copy(main_ref, mains, sem_in.at[0]),
            pltpu.make_async_copy(back_ref, backs, sem_in.at[1]),
            pltpu.make_async_copy(rows_ref, held.at[:, :, :width], sem_in.at[2]),
        ]
        for copy in loads:
            copy.start()
        for copy in loads:
            copy.wait()
        stores = []
        for k in range(blocks):
            i = core ^ k
            near = jnp.where(i >= base, 1.0, 0.0)
            term = backs[jnp.maximum(i - base, 0)].astype(F32) * near
            held[k, :, width : width + DH] = (mains[i, :, :DH] * scale + term[:, :DH]).astype(BF16)
            held[k, :, width + DH :] = (mains[i, :, DH:] + term[:, DH:]).astype(BF16)
            copy = pltpu.make_async_copy(held.at[k], outs[k], sem_out.at[k])
            copy.start()
            stores.append(copy)
        for copy in stores:
            copy.wait()

    total = width + 2 * DH
    return pl.pallas_call(
        kernel,
        in_specs=[pl.BlockSpec(memory_space=pltpu.SMEM)] + [ANY] * 3,
        out_specs=[ANY] * blocks,
        out_shape=[jax.ShapeDtypeStruct((BLOCK, total), BF16)] * blocks,
        scratch_shapes=[
            pltpu.VMEM((blocks, BLOCK, total), BF16),
            pltpu.VMEM((blocks, BLOCK, 2 * DH), F32),
            pltpu.VMEM((HALO, BLOCK, 2 * DH), BF16),
            pltpu.SemaphoreType.DMA((3,)),
            pltpu.SemaphoreType.DMA((blocks,)),
        ],
        cost_estimate=pl.CostEstimate(flops=0, bytes_accessed=5 << 20, transcendentals=0),
        compiler_params=pltpu.CompilerParams(vmem_limit_bytes=62 << 20),
        name="finish",
    )(core_index, rows, main, back)


def place_rows(block_index, arrived, last_rows, groups):
    repeats = groups // KVH
    width = QH // groups * DH
    half = width // CHUNKS
    first_row = arrived.shape[1] - BLOCK

    def kernel(*refs):
        at_ref, arrived_ref, *refs = refs
        lasts, refs = refs[:groups], refs[groups:]
        gq_ref, gk_ref, gv_ref, rows, held, sums, sem_in, sem_out = refs
        at = at_ref[0]
        loads, stores = [], []

        def load(src, dst):
            copy = pltpu.make_async_copy(src, dst, sem_in.at[len(loads)])
            copy.start()
            loads.append(copy)

        def store(src, dst):
            copy = pltpu.make_async_copy(src, dst, sem_out.at[len(stores)])
            copy.start()
            stores.append(copy)

        for r in range(groups):
            load(arrived_ref.at[r, first_row:, :], rows.at[:, r * width : r * width + half])
        for k in range(groups):
            group = at ^ k
            col = pl.multiple_of(group * width + half, half)
            load(lasts[k].at[:, :half], rows.at[:, pl.ds(col, half)])
            load(lasts[k].at[:, half:], held.at[group])
        for copy in loads:
            copy.wait()
        store(rows, gq_ref)
        for head in range(KVH):
            total = held[head * repeats].astype(F32)
            for extra in range(1, repeats):
                total += held[head * repeats + extra].astype(F32)
            sums[0, :, head * DH : (head + 1) * DH] = total[:, :DH].astype(BF16)
            sums[1, :, head * DH : (head + 1) * DH] = total[:, DH:].astype(BF16)
        store(sums.at[0], gk_ref)
        store(sums.at[1], gv_ref)
        for copy in stores:
            copy.wait()

    return pl.pallas_call(
        kernel,
        in_specs=[pl.BlockSpec(memory_space=pltpu.SMEM)] + [ANY] * (groups + 1),
        out_specs=[ANY] * 3,
        out_shape=[
            jax.ShapeDtypeStruct((BLOCK, QH * DH), BF16),
            jax.ShapeDtypeStruct((BLOCK, KVH * DH), BF16),
            jax.ShapeDtypeStruct((BLOCK, KVH * DH), BF16),
        ],
        scratch_shapes=[
            pltpu.VMEM((BLOCK, QH * DH), BF16),
            pltpu.VMEM((groups, BLOCK, 2 * DH), BF16),
            pltpu.VMEM((2, BLOCK, KVH * DH), BF16),
            pltpu.SemaphoreType.DMA((3 * groups,)),
            pltpu.SemaphoreType.DMA((3,)),
        ],
        cost_estimate=pl.CostEstimate(flops=0, bytes_accessed=6 << 20, transcendentals=0),
        compiler_params=pltpu.CompilerParams(vmem_limit_bytes=62 << 20),
        name="place_rows",
    )(block_index, arrived, *last_rows)


def place_out(parts, rows, chunk, held):
    groups, _, half = parts.shape

    def kernel(*refs):
        in_ref, (out_ref, buf, sem_in, sem_out) = refs[0], refs[-4:]
        loads = [
            pltpu.make_async_copy(in_ref.at[r, :rows, :], buf.at[r], sem_in.at[r])
            for r in range(groups)
        ]
        stores = []
        for copy in loads:
            copy.start()
        for r in range(groups):
            col = (r * CHUNKS + chunk) * half
            loads[r].wait()
            copy = pltpu.make_async_copy(buf.at[r], out_ref.at[:, col : col + half], sem_out.at[r])
            copy.start()
            stores.append(copy)
        for copy in stores:
            copy.wait()

    operands = [parts] if held is None else [parts, held]
    return pl.pallas_call(
        kernel,
        in_specs=[ANY] * len(operands),
        out_specs=ANY,
        out_shape=jax.ShapeDtypeStruct((rows, QH * DH), BF16),
        scratch_shapes=[
            pltpu.VMEM((groups, rows, half), BF16),
            pltpu.SemaphoreType.DMA((groups,)),
            pltpu.SemaphoreType.DMA((groups,)),
        ],
        input_output_aliases={} if held is None else {1: 0},
        cost_estimate=pl.CostEstimate(
            flops=0, bytes_accessed=4 * groups * rows * half, transcendentals=0
        ),
        compiler_params=pltpu.CompilerParams(vmem_limit_bytes=62 << 20),
        name="place_out",
    )(*operands)


def body(shape, query_rows, key_rows, value_rows, grad_out, doc_ids, route_table):
    n_seq, n_plane, per_plane = shape
    groups = n_seq * per_plane
    blocks = n_plane * per_plane
    slots = route_table.shape[1] * route_table.shape[2]
    axes = ("seq", "hs", "hp")
    plane_axes = ("seq", "hp")
    seq_at = lax.axis_index("seq")
    plane = lax.axis_index("hs")
    part = lax.axis_index("hp")
    core = seq_at * per_plane + part

    def device(seq, hs, hp):
        return (seq * n_plane + hs) * per_plane + hp

    every = [(a, b, c) for a in range(n_seq) for b in range(n_plane) for c in range(per_plane)]

    def swap(x):
        return lax.all_to_all(x, plane_axes, split_axis=0, concat_axis=0, tiled=True)

    def along(x, k):
        return lax.ppermute(x, axes, [(device(a, b, c), device(a, b ^ k, c)) for a, b, c in every])

    def home(x, k):
        pairs = []
        for a, b, c in every:
            index = (a * per_plane + c) ^ k
            pairs.append((device(a, b, c), device(b, index // per_plane, index % per_plane)))
        return lax.ppermute(x, axes, pairs)

    routes = lax.dynamic_index_in_dim(route_table, plane, 0, keepdims=False).reshape(slots)
    match = routes[None, :] == jnp.arange(blocks, dtype=jnp.int32)[:, None]
    slot_of = jnp.sum(jnp.where(match, jnp.arange(slots, dtype=jnp.int32)[None, :], 0), axis=1)
    docs_pad = jnp.concatenate([jnp.full((HALO,), -1, jnp.int32), doc_ids])
    docs = lax.dynamic_slice_in_dim(docs_pad, plane * blocks, blocks + HALO, 0)
    own = docs[HALO:]
    counts = sum(
        (docs[HALO - d : HALO - d + blocks] == own).astype(jnp.int32) for d in range(DOCMAX)
    )
    live = (routes < blocks).astype(jnp.int32)
    table = jnp.concatenate(
        [slot_of, counts, jnp.stack([plane, core]).astype(jnp.int32), live]
    )

    def spread(x):
        return x.reshape((n_seq, per_plane) + x.shape[1:])

    def by_slot(x):
        return x.reshape(slots, BLOCK, x.shape[-1])

    first_pack = pack_first(query_rows, key_rows, value_rows, groups)
    first_plane = spread(swap(first_pack))
    grad_pack = pack_half(grad_out, 0, groups)
    grad_pack_second = pack_half(grad_out, 1, groups)
    width = grad_pack.shape[-1]

    plane_index = plane.astype(jnp.int32).reshape(1)
    kv_parts, query_parts = relay_in(plane_index, first_plane, width)
    for k in range(1, n_plane):
        kv_parts[k] = along(kv_parts[k], k)
    for k in range(1, n_plane):
        query_parts[k] = along(query_parts[k], k)
    grad_first = by_slot(swap(grad_pack))
    grad_second = by_slot(swap(grad_pack_second))

    rows = grad_out.shape[0]
    out_first, *rows_first, carried = attend(
        table, kv_parts, None, grad_first, None, False, blocks, (groups, rows)
    )
    for k in range(1, n_plane):
        rows_first[k] = along(rows_first[k], k)
    back_first = swap(out_first)
    out_second, rows_second, main, back = attend(
        table, kv_parts, query_parts, grad_second, carried, True, blocks, (groups, rows + BLOCK)
    )
    down = [(device(a, b, c), device(a, b - 1, c)) for a, b, c in every if b]
    back = lax.ppermute(back, axes, down)
    out_second = relay_out(plane_index, rows_first, out_second)
    back_second = swap(out_second)
    rows_second = finish(core.astype(jnp.int32).reshape(1), rows_second, main, back)
    home_second = []
    for k in range(blocks):
        home_second.append(home(rows_second[k], k))

    attn_out = place_out(back_first, rows, 0, None)
    block_index = (plane * per_plane + part).astype(jnp.int32).reshape(1)
    grad_query, grad_key, grad_value = place_rows(
        block_index, back_second, home_second, groups
    )
    attn_out = place_out(back_second, rows, 1, attn_out)
    return (attn_out, grad_query, grad_key, grad_value)


def whole(shape, *args):
    return body(shape, *args)


def solution(mesh):
    n_seq, n_head = mesh.shape["seq"], mesh.shape["head"]
    per_plane = n_head // n_seq
    shape = (n_seq, n_seq, per_plane)
    wide = Mesh(mesh.devices.reshape(shape), ("seq", "hs", "hp"))
    rows = P(("seq", "hs", "hp"), None)
    return jax.shard_map(
        functools.partial(whole, shape),
        mesh=wide,
        in_specs=(rows, rows, rows, rows, P(), P()),
        out_specs=(rows, rows, rows, rows),
        check_vma=False,
    )
```

profile of v0, /device:TPU:17, one launch (start us, length us, event | category | flops | bytes accessed | tf_op | source)
XLA Modules:
  0.0 296.5 jit_solution(18443610373231396587)
XLA Ops:
  0.6 2.4 shard_map.94
  3.1 4.9 %all-to-all-start.1 = ((bf16[8,256,512]{2,1,0:T(8,128)(2,1)}), bf16[8,256,512]{2,1,0:T(8,128)(2,1)}, u32[]{:S(2)}, u32[]{:S(2)}) async-start(bf16[8,256,512]{2,1,0:T(8,128)(2,1)} %shard_map.94), calls=%async_computation.1 | async-start | bytes 4194304 | tf_op jit(solution)/shard_map/all_to_all | solution.py:566
  8.0 2.7 shard_map.93
  10.7 22.7 %all-to-all-done.1 = bf16[8,256,512]{2,1,0:T(8,128)(2,1)} async-done(((bf16[8,256,512]{2,1,0:T(8,128)(2,1)}), bf16[8,256,512]{2,1,0:T(8,128)(2,1)}, u32[]{:S(2)}, u32[]{:S(2)}) %all-to-all-start.1) | async-done | bytes 2097184 | tf_op jit(solution)/shard_map/all_to_all | solution.py:566
  33.4 5.1 %all-to-all-start = ((bf16[8,128,1280]{2,1,0:T(8,128)(2,1)}), bf16[8,128,1280]{2,1,0:T(8,128)(2,1)}, u32[]{:S(2)}, u32[]{:S(2)}) async-start(bf16[8,128,1280]{2,1,0:T(8,128)(2,1)} %shard_map.93), calls=%async_computation | async-start | bytes 5242880 | tf_op jit(solution)/shard_map/all_to_all | solution.py:566
  38.5 2.4 shard_map.95
  40.9 28.6 %all-to-all-done = bf16[8,128,1280]{2,1,0:T(8,128)(2,1)} async-done(((bf16[8,128,1280]{2,1,0:T(8,128)(2,1)}), bf16[8,128,1280]{2,1,0:T(8,128)(2,1)}, u32[]{:S(2)}, u32[]{:S(2)}) %all-to-all-start) | async-done | bytes 2621472 | tf_op jit(solution)/shard_map/all_to_all | solution.py:566
  69.5 5.0 %all-to-all-start.2 = ((bf16[8,256,512]{2,1,0:T(8,128)(2,1)}), bf16[8,256,512]{2,1,0:T(8,128)(2,1)}, u32[]{:S(2)}, u32[]{:S(2)}) async-start(bf16[8,256,512]{2,1,0:T(8,128)(2,1)} %shard_map.95), calls=%async_computation.2 | async-start | bytes 4194304 | tf_op jit(solution)/shard_map/all_to_all | solution.py:566
  74.7 3.0 %relay_in.1 = (bf16[2,128,1024]{2,1,0:T(8,128)(2,1)}, bf16[2,128,1024]{2,1,0:T(8,128)(2,1)}, bf16[2,128,1024]{2,1,0:T(8,128)(2,1)}, bf16[2,128,1024]{2,1,0:T(8,1...) custom-call(s32[1]{0:T(128)} %bitcast.plane_ref, ...), custom_call_target="tpu_custom_call" | custom-call | bytes 6291456 | tf_op jit(solution)/shard_map/relay_in/pallas_call | solution.py:121
  77.8 1.4 collective-permute-start
  79.2 1.3 collective-permute-start.2
  80.6 0.6 concatenate.7.refs_0_
  81.2 19.3 %collective-permute-done.refs_2_ = bf16[2,128,1024]{2,1,0:T(8,128)(2,1)S(1)} collective-permute-done((bf16[2,128,1024]{2,1,0:T(8,128)(2,1)}, bf16[2,128,1024]{2,1,0:T(8,128)(2,1)S(1)}, u32[]{:S(2)}, u32[]{:S(2)}) %collective-permute-start) | collective-permute-done | bytes 524320 | tf_op jit(solution)/shard_map/ppermute | solution.py:569
  100.6 2.0 collective-permute-done.1.refs_3_
  102.5 23.5 %collective-permute-done.2.refs_4_ = bf16[2,128,1024]{2,1,0:T(8,128)(2,1)S(1)} collective-permute-done((bf16[2,128,1024]{2,1,0:T(8,128)(2,1)}, bf16[2,128,1024]{2,1,0:T(8,128)(2,1)S(1)}, u32[]{:S(2)}, u32[]{:S(2)}) %collective-permute-start.2) | collective-permute-done | bytes 524320 | tf_op jit(solution)/shard_map/ppermute | solution.py:569
  126.0 0.8 copy-done.15
  126.8 17.8 %attend_first.1 = (bf16[8,256,512]{2,1,0:T(8,128)(2,1)}, bf16[2,128,512]{2,1,0:T(8,128)(2,1)}, bf16[2,128,512]{2,1,0:T(8,128)(2,1)}, bf16[2,128,512]{2,1,0:T(8,1...) custom-call(s32[34]{0:T(128)} %concatenate.7.refs_0_, bf16[2,128,1024]{2,1,0:T(8,128)(2,1)} %get-tuple-element.33.refs_1_, ...), custom_call_target="tpu_custom_call" | custom-call | flops 2684354560 | bytes 12582912 | tf_op jit(solution)/shard_map/attend_first/pallas_call | solution.py:377
  144.7 5.7 %all-to-all-start.4 = ((bf16[8,256,512]{2,1,0:T(8,128)(2,1)}), bf16[8,256,512]{2,1,0:T(8,128)(2,1)}, u32[]{:S(2)}, u32[]{:S(2)}) async-start(bf16[8,256,512]{2,1,0:T(8,128)(2,1)} %get-tuple-element.47), calls=%async_computation.4 | async-start | bytes 4194304 | tf_op jit(solution)/shard_map/all_to_all | solution.py:566
  150.4 4.3 %collective-permute-start.7 = (bf16[2,128,512]{2,1,0:T(8,128)(2,1)S(1)}, bf16[2,128,512]{2,1,0:T(8,128)(2,1)S(1)}, u32[]{:S(2)}, u32[]{:S(2)}) collective-permute-start(bf16[2,128,512]{2,1,0:T(8,128)(2,1)S(1)} %copy-done.18), channel_id=1, source_target_pairs={{0,4},{1,5},{2,6},{3,7},{4,0},{5,1},{6,2},{7,3},{8,12},{9,13},{10,... | collective-permute-start | bytes 786440 | tf_op jit(solution)/shard_map/ppermute | solution.py:569
  154.8 1.2 collective-permute-start.3
  156.0 1.4 collective-permute-start.4
  157.4 4.2 %collective-permute-done.6.refs_6_ = bf16[2,128,512]{2,1,0:T(8,128)(2,1)S(1)} collective-permute-done((bf16[2,128,512]{2,1,0:T(8,128)(2,1)S(1)}, bf16[2,128,512]{2,1,0:T(8,128)(2,1)S(1)}, u32[]{:S(2)}, u32[]{:S(2)}) %collective-permute-start.6) | collective-permute-done | bytes 262176 | tf_op jit(solution)/shard_map/ppermute | solution.py:569
  161.6 9.5 %collective-permute-done.7.refs_7_ = bf16[2,128,512]{2,1,0:T(8,128)(2,1)S(1)} collective-permute-done((bf16[2,128,512]{2,1,0:T(8,128)(2,1)S(1)}, bf16[2,128,512]{2,1,0:T(8,128)(2,1)S(1)}, u32[]{:S(2)}, u32[]{:S(2)}) %collective-permute-start.7) | collective-permute-done | bytes 262176 | tf_op jit(solution)/shard_map/ppermute | solution.py:569
  171.1 16.9 %collective-permute-done.8.refs_8_ = bf16[2,128,512]{2,1,0:T(8,128)(2,1)S(1)} collective-permute-done((bf16[2,128,512]{2,1,0:T(8,128)(2,1)S(1)}, bf16[2,128,512]{2,1,0:T(8,128)(2,1)S(1)}, u32[]{:S(2)}, u32[]{:S(2)}) %collective-permute-start.8) | collective-permute-done | bytes 262176 | tf_op jit(solution)/shard_map/ppermute | solution.py:569
  188.0 0.7 copy-done.25
  188.7 18.4 %attend_last.1 = (bf16[8,384,512]{2,1,0:T(8,128)(2,1)}, bf16[8,128,512]{2,1,0:T(8,128)(2,1)}, f32[8,128,256]{2,1,0:T(8,128)}, bf16[6,128,256]{2,1,0:T(8,128)(2,1)}) custom-call(s32[34]{0:T(128)} %concatenate.7.refs_0_, bf16[2,128,1024]{2,1,0:T(8,128)(2,1)} %get-tuple-element.33.refs_1_, bf16[2,128,1024]{2,1,0:T(8,128)(2,1)} %copy-done.13, ...), custom_call_target="tpu_custom_call" | custom-call | flops 2684354560 | bytes 12582912 | tf_op jit(solution)/shard_map/attend_last/pallas_call | solution.py:377
  207.2 0.6 copy-done.2
  208.0 2.0 relay_out.1
  210.1 7.0 %all-to-all-start.3 = ((bf16[8,384,512]{2,1,0:T(8,128)(2,1)}), bf16[8,384,512]{2,1,0:T(8,128)(2,1)}, u32[]{:S(2)}, u32[]{:S(2)}) async-start(bf16[8,384,512]{2,1,0:T(8,128)(2,1)} %relay_out.1), calls=%async_computation.3 | async-start | bytes 6291456 | tf_op jit(solution)/shard_map/all_to_all | solution.py:566
  217.1 7.1 %collective-permute-start.9 = (bf16[6,128,256]{2,1,0:T(8,128)(2,1)S(1)}, bf16[6,128,256]{2,1,0:T(8,128)(2,1)S(1)}, u32[]{:S(2)}, u32[]{:S(2)}) collective-permute-start(bf16[6,128,256]{2,1,0:T(8,128)(2,1)S(1)} %copy-done.16), channel_id=1, source_target_pairs={{2,0},{3,1},{4,2},{5,3},{6,4},{7,5},{10,8},{11,9},{12,10},{13,11},... | collective-permute-start | bytes 1179656 | tf_op jit(solution)/shard_map/ppermute | solution.py:624
  224.2 8.3 %collective-permute-done.9.back_ref = bf16[6,128,256]{2,1,0:T(8,128)(2,1)S(1)} collective-permute-done((bf16[6,128,256]{2,1,0:T(8,128)(2,1)S(1)}, bf16[6,128,256]{2,1,0:T(8,128)(2,1)S(1)}, u32[]{:S(2)}, u32[]{:S(2)}) %collective-permute-start.9) | collective-permute-done | bytes 393248 | tf_op jit(solution)/shard_map/ppermute | solution.py:624
  232.5 0.7 copy-done.1
  233.3 2.9 finish.1
  236.2 6.1 %collective-permute-start.10 = (bf16[128,768]{1,0:T(8,128)(2,1)}, bf16[128,768]{1,0:T(8,128)(2,1)S(1)}, u32[]{:S(2)}, u32[]{:S(2)}) collective-permute-start(bf16[128,768]{1,0:T(8,128)(2,1)} %get-tuple-element.51), channel_id=1, source_target_pairs={{0,0},{1,1},{2,8},{3,9},{4,16},{5,17},{6,24},{7,25},{8,2},{9,3},{1... | collective-permute-start | bytes 589832 | tf_op jit(solution)/shard_map/ppermute | solution.py:576
  242.3 1.0 collective-permute-start.11
  243.3 3.5 %collective-permute-start.12 = (bf16[128,768]{1,0:T(8,128)(2,1)}, bf16[128,768]{1,0:T(8,128)(2,1)S(1)}, u32[]{:S(2)}, u32[]{:S(2)}) collective-permute-start(bf16[128,768]{1,0:T(8,128)(2,1)} %get-tuple-element.53), channel_id=1, source_target_pairs={{0,2},{1,3},{2,10},{3,11},{4,18},{5,19},{6,26},{7,27},{8,0},{9,1},... | collective-permute-start | bytes 589832 | tf_op jit(solution)/shard_map/ppermute | solution.py:576
  247.0 17.0 %collective-permute-done.10.refs_2_ = bf16[128,768]{1,0:T(8,128)(2,1)S(1)} collective-permute-done((bf16[128,768]{1,0:T(8,128)(2,1)}, bf16[128,768]{1,0:T(8,128)(2,1)S(1)}, u32[]{:S(2)}, u32[]{:S(2)}) %collective-permute-start.10) | collective-permute-done | bytes 196640 | tf_op jit(solution)/shard_map/ppermute | solution.py:576
  264.1 4.8 %collective-permute-done.11.refs_3_ = bf16[128,768]{1,0:T(8,128)(2,1)S(1)} collective-permute-done((bf16[128,768]{1,0:T(8,128)(2,1)}, bf16[128,768]{1,0:T(8,128)(2,1)S(1)}, u32[]{:S(2)}, u32[]{:S(2)}) %collective-permute-start.11) | collective-permute-done | bytes 196640 | tf_op jit(solution)/shard_map/ppermute | solution.py:576
  268.9 1.0 collective-permute-start.16
  269.9 2.7 collective-permute-done.12.refs_4_
  272.6 0.4 collective-permute-start.17
  273.0 2.4 place_out.2.refs_1_
  275.4 2.4 place_out.3
  277.9 5.9 %collective-permute-done.15.refs_7_ = bf16[128,768]{1,0:T(8,128)(2,1)S(1)} collective-permute-done((bf16[128,768]{1,0:T(8,128)(2,1)}, bf16[128,768]{1,0:T(8,128)(2,1)S(1)}, u32[]{:S(2)}, u32[]{:S(2)}) %collective-permute-start.15) | collective-permute-done | bytes 196640 | tf_op jit(solution)/shard_map/ppermute | solution.py:576
  283.7 3.3 %collective-permute-done.16.refs_8_ = bf16[128,768]{1,0:T(8,128)(2,1)S(1)} collective-permute-done((bf16[128,768]{1,0:T(8,128)(2,1)}, bf16[128,768]{1,0:T(8,128)(2,1)S(1)}, u32[]{:S(2)}, u32[]{:S(2)}) %collective-permute-start.16) | collective-permute-done | bytes 196640 | tf_op jit(solution)/shard_map/ppermute | solution.py:576
  287.0 5.2 %collective-permute-done.17.refs_9_ = bf16[128,768]{1,0:T(8,128)(2,1)S(1)} collective-permute-done((bf16[128,768]{1,0:T(8,128)(2,1)}, bf16[128,768]{1,0:T(8,128)(2,1)S(1)}, u32[]{:S(2)}, u32[]{:S(2)}) %collective-permute-start.17) | collective-permute-done | bytes 196640 | tf_op jit(solution)/shard_map/ppermute | solution.py:576
  292.3 0.7 copy-done.12
  292.9 3.5 %place_rows.1 = (bf16[128,8192]{1,0:T(8,128)(2,1)}, bf16[128,1024]{1,0:T(8,128)(2,1)}, bf16[128,1024]{1,0:T(8,128)(2,1)}) custom-call(s32[1]{0:T(128)} %bitcast.5.refs_0_, bf16[8,384,512]{2,1,0:T(8,128)(2,1)} %all-to-all-done.3.refs_0_.refs_1_, bf16[128,768]{1,0:T(8,128)(2,1)} %copy-done.5, bf16[128,768]{1,0:T(8,128)(2,1)} %copy-done.6, ...), custom_call_target="tpu_custom_call" | custom-call | bytes 6291456 | tf_op jit(solution)/shard_map/place_rows/pallas_call | solution.py:485
  (70 shorter events, 1.0 us)
Async XLA Ops:
  0.6 73.9 %copy-start = (s32[4,4,4]{2,1,0:T(4,128)S(1)}, s32[4,4,4]{2,1,0:T(4,128)}, u32[]{:S(2)}) copy-start(s32[4,4,4]{2,1,0:T(4,128)} %param.11) | copy-start | bytes 772
  3.1 30.3 %all-to-all-start.1 = ((bf16[8,256,512]{2,1,0:T(8,128)(2,1)}), bf16[8,256,512]{2,1,0:T(8,128)(2,1)}, u32[]{:S(2)}, u32[]{:S(2)}) async-start(bf16[8,256,512]{2,1,0:T(8,128)(2,1)} %shard_map.94), calls=%async_computation.1 | async-start | bytes 4194304 | tf_op jit(solution)/shard_map/all_to_all | solution.py:566
  33.4 36.1 %all-to-all-start = ((bf16[8,128,1280]{2,1,0:T(8,128)(2,1)}), bf16[8,128,1280]{2,1,0:T(8,128)(2,1)}, u32[]{:S(2)}, u32[]{:S(2)}) async-start(bf16[8,128,1280]{2,1,0:T(8,128)(2,1)} %shard_map.93), calls=%async_computation | async-start | bytes 5242880 | tf_op jit(solution)/shard_map/all_to_all | solution.py:566
  69.5 75.1 %all-to-all-start.2 = ((bf16[8,256,512]{2,1,0:T(8,128)(2,1)}), bf16[8,256,512]{2,1,0:T(8,128)(2,1)}, u32[]{:S(2)}, u32[]{:S(2)}) async-start(bf16[8,256,512]{2,1,0:T(8,128)(2,1)} %shard_map.95), calls=%async_computation.2 | async-start | bytes 4194304 | tf_op jit(solution)/shard_map/all_to_all | solution.py:566
  74.5 6.0 %copy-start.26 = (s32[32]{0:T(128)S(1)}, s32[32]{0:T(128)}, u32[]{:S(2)}) copy-start(s32[32]{0:T(128)} %param.10) | copy-start | bytes 388
  77.8 22.8 %collective-permute-start = (bf16[2,128,1024]{2,1,0:T(8,128)(2,1)}, bf16[2,128,1024]{2,1,0:T(8,128)(2,1)S(1)}, u32[]{:S(2)}, u32[]{:S(2)}) collective-permute-start(bf16[2,128,1024]{2,1,0:T(8,128)(2,1)} %get-tuple-element.34), channel_id=1, source_target_pairs={{0,2},{1,3},{2,0},{3,1},{4,6},{5,7},{6,4},{7,5},{8,10},{9,11},{10,... | collective-permute-start | bytes 1572872 | tf_op jit(solution)/shard_map/ppermute | solution.py:569
  79.1 23.4 %collective-permute-start.1 = (bf16[2,128,1024]{2,1,0:T(8,128)(2,1)}, bf16[2,128,1024]{2,1,0:T(8,128)(2,1)S(1)}, u32[]{:S(2)}, u32[]{:S(2)}) collective-permute-start(bf16[2,128,1024]{2,1,0:T(8,128)(2,1)} %get-tuple-element.35), channel_id=1, source_target_pairs={{0,4},{1,5},{2,6},{3,7},{4,0},{5,1},{6,2},{7,3},{8,12},{9,13},{10,... | collective-permute-start | bytes 1572872 | tf_op jit(solution)/shard_map/ppermute | solution.py:569
  79.2 46.8 %collective-permute-start.2 = (bf16[2,128,1024]{2,1,0:T(8,128)(2,1)}, bf16[2,128,1024]{2,1,0:T(8,128)(2,1)S(1)}, u32[]{:S(2)}, u32[]{:S(2)}) collective-permute-start(bf16[2,128,1024]{2,1,0:T(8,128)(2,1)} %get-tuple-element.36), channel_id=1, source_target_pairs={{0,6},{1,7},{2,4},{3,5},{4,2},{5,3},{6,0},{7,1},{8,14},{9,15},{10,... | collective-permute-start | bytes 1572872 | tf_op jit(solution)/shard_map/ppermute | solution.py:569
  100.5 25.5 %copy-start.13 = (bf16[2,128,1024]{2,1,0:T(8,128)(2,1)}, bf16[2,128,1024]{2,1,0:T(8,128)(2,1)S(1)}, u32[]{:S(2)}) copy-start(bf16[2,128,1024]{2,1,0:T(8,128)(2,1)S(1)} %collective-permute-done.refs_2_) | copy-start | bytes 1572868
  102.5 23.5 %copy-start.14 = (bf16[2,128,1024]{2,1,0:T(8,128)(2,1)}, bf16[2,128,1024]{2,1,0:T(8,128)(2,1)S(1)}, u32[]{:S(2)}) copy-start(bf16[2,128,1024]{2,1,0:T(8,128)(2,1)S(1)} %collective-permute-done.1.refs_3_) | copy-start | bytes 1572868
  126.0 0.8 copy-start.15
  144.7 5.7 %copy-start.19 = (bf16[2,128,512]{2,1,0:T(8,128)(2,1)S(1)}, bf16[2,128,512]{2,1,0:T(8,128)(2,1)}, u32[]{:S(2)}) copy-start(bf16[2,128,512]{2,1,0:T(8,128)(2,1)} %get-tuple-element.42) | copy-start | bytes 786436
  144.7 5.7 %copy-start.18 = (bf16[2,128,512]{2,1,0:T(8,128)(2,1)S(1)}, bf16[2,128,512]{2,1,0:T(8,128)(2,1)}, u32[]{:S(2)}) copy-start(bf16[2,128,512]{2,1,0:T(8,128)(2,1)} %get-tuple-element.43) | copy-start | bytes 786436
  144.7 10.1 %copy-start.17 = (bf16[2,128,512]{2,1,0:T(8,128)(2,1)S(1)}, bf16[2,128,512]{2,1,0:T(8,128)(2,1)}, u32[]{:S(2)}) copy-start(bf16[2,128,512]{2,1,0:T(8,128)(2,1)} %get-tuple-element.44) | copy-start | bytes 786436
  144.7 10.1 %copy-start.22 = (bf16[2,128,512]{2,1,0:T(8,128)(2,1)S(1)}, bf16[2,128,512]{2,1,0:T(8,128)(2,1)}, u32[]{:S(2)}) copy-start(bf16[2,128,512]{2,1,0:T(8,128)(2,1)} %get-tuple-element.38) | copy-start | bytes 786436
  144.7 11.3 %copy-start.21 = (bf16[2,128,512]{2,1,0:T(8,128)(2,1)S(1)}, bf16[2,128,512]{2,1,0:T(8,128)(2,1)}, u32[]{:S(2)}) copy-start(bf16[2,128,512]{2,1,0:T(8,128)(2,1)} %get-tuple-element.39) | copy-start | bytes 786436
  144.7 16.9 %copy-start.20 = (bf16[2,128,512]{2,1,0:T(8,128)(2,1)S(1)}, bf16[2,128,512]{2,1,0:T(8,128)(2,1)}, u32[]{:S(2)}) copy-start(bf16[2,128,512]{2,1,0:T(8,128)(2,1)} %get-tuple-element.40) | copy-start | bytes 786436
  144.7 65.3 %all-to-all-start.4 = ((bf16[8,256,512]{2,1,0:T(8,128)(2,1)}), bf16[8,256,512]{2,1,0:T(8,128)(2,1)}, u32[]{:S(2)}, u32[]{:S(2)}) async-start(bf16[8,256,512]{2,1,0:T(8,128)(2,1)} %get-tuple-element.47), calls=%async_computation.4 | async-start | bytes 4194304 | tf_op jit(solution)/shard_map/all_to_all | solution.py:566
  150.4 11.2 %collective-permute-start.6 = (bf16[2,128,512]{2,1,0:T(8,128)(2,1)S(1)}, bf16[2,128,512]{2,1,0:T(8,128)(2,1)S(1)}, u32[]{:S(2)}, u32[]{:S(2)}) collective-permute-start(bf16[2,128,512]{2,1,0:T(8,128)(2,1)S(1)} %copy-done.19), channel_id=1, source_target_pairs={{0,2},{1,3},{2,0},{3,1},{4,6},{5,7},{6,4},{7,5},{8,10},{9,11},{10,... | collective-permute-start | bytes 786440 | tf_op jit(solution)/shard_map/ppermute | solution.py:569
  150.4 20.7 %collective-permute-start.7 = (bf16[2,128,512]{2,1,0:T(8,128)(2,1)S(1)}, bf16[2,128,512]{2,1,0:T(8,128)(2,1)S(1)}, u32[]{:S(2)}, u32[]{:S(2)}) collective-permute-start(bf16[2,128,512]{2,1,0:T(8,128)(2,1)S(1)} %copy-done.18), channel_id=1, source_target_pairs={{0,4},{1,5},{2,6},{3,7},{4,0},{5,1},{6,2},{7,3},{8,12},{9,13},{10,... | collective-permute-start | bytes 786440 | tf_op jit(solution)/shard_map/ppermute | solution.py:569
  154.8 33.2 %collective-permute-start.8 = (bf16[2,128,512]{2,1,0:T(8,128)(2,1)S(1)}, bf16[2,128,512]{2,1,0:T(8,128)(2,1)S(1)}, u32[]{:S(2)}, u32[]{:S(2)}) collective-permute-start(bf16[2,128,512]{2,1,0:T(8,128)(2,1)S(1)} %copy-done.17), channel_id=1, source_target_pairs={{0,6},{1,7},{2,4},{3,5},{4,2},{5,3},{6,0},{7,1},{8,14},{9,15},{10,... | collective-permute-start | bytes 786440 | tf_op jit(solution)/shard_map/ppermute | solution.py:569
  154.8 52.4 %collective-permute-start.3 = (bf16[2,128,512]{2,1,0:T(8,128)(2,1)S(1)}, bf16[2,128,512]{2,1,0:T(8,128)(2,1)S(1)}, u32[]{:S(2)}, u32[]{:S(2)}) collective-permute-start(bf16[2,128,512]{2,1,0:T(8,128)(2,1)S(1)} %copy-done.22), channel_id=1, source_target_pairs={{0,2},{1,3},{2,0},{3,1},{4,6},{5,7},{6,4},{7,5},{8,10},{9,11},{10,... | collective-permute-start | bytes 786440 | tf_op jit(solution)/shard_map/ppermute | solution.py:569
  156.0 51.1 %collective-permute-start.4 = (bf16[2,128,512]{2,1,0:T(8,128)(2,1)S(1)}, bf16[2,128,512]{2,1,0:T(8,128)(2,1)S(1)}, u32[]{:S(2)}, u32[]{:S(2)}) collective-permute-start(bf16[2,128,512]{2,1,0:T(8,128)(2,1)S(1)} %copy-done.21), channel_id=1, source_target_pairs={{0,4},{1,5},{2,6},{3,7},{4,0},{5,1},{6,2},{7,3},{8,12},{9,13},{10,... | collective-permute-start | bytes 786440 | tf_op jit(solution)/shard_map/ppermute | solution.py:569
  161.6 27.2 %copy-start.23 = (bf16[2,128,512]{2,1,0:T(8,128)(2,1)}, bf16[2,128,512]{2,1,0:T(8,128)(2,1)S(1)}, u32[]{:S(2)}) copy-start(bf16[2,128,512]{2,1,0:T(8,128)(2,1)S(1)} %collective-permute-done.6.refs_6_) | copy-start | bytes 786436
  161.6 45.6 %collective-permute-start.5 = (bf16[2,128,512]{2,1,0:T(8,128)(2,1)S(1)}, bf16[2,128,512]{2,1,0:T(8,128)(2,1)S(1)}, u32[]{:S(2)}, u32[]{:S(2)}) collective-permute-start(bf16[2,128,512]{2,1,0:T(8,128)(2,1)S(1)} %copy-done.20), channel_id=1, source_target_pairs={{0,6},{1,7},{2,4},{3,5},{4,2},{5,3},{6,0},{7,1},{8,14},{9,15},{10,... | collective-permute-start | bytes 786440 | tf_op jit(solution)/shard_map/ppermute | solution.py:569
  171.1 16.9 %copy-start.24 = (bf16[2,128,512]{2,1,0:T(8,128)(2,1)}, bf16[2,128,512]{2,1,0:T(8,128)(2,1)S(1)}, u32[]{:S(2)}) copy-start(bf16[2,128,512]{2,1,0:T(8,128)(2,1)S(1)} %collective-permute-done.7.refs_7_) | copy-start | bytes 786436
  188.0 0.7 copy-start.25
  207.2 0.8 copy-start.3
  207.2 0.8 copy-start.4
  210.0 7.1 %copy-start.16 = (bf16[6,128,256]{2,1,0:T(8,128)(2,1)S(1)}, bf16[6,128,256]{2,1,0:T(8,128)(2,1)}, u32[]{:S(2)}) copy-start(bf16[6,128,256]{2,1,0:T(8,128)(2,1)} %get-tuple-element.50) | copy-start | bytes 1179652
  210.1 65.3 %all-to-all-start.3 = ((bf16[8,384,512]{2,1,0:T(8,128)(2,1)}), bf16[8,384,512]{2,1,0:T(8,128)(2,1)}, u32[]{:S(2)}, u32[]{:S(2)}) async-start(bf16[8,384,512]{2,1,0:T(8,128)(2,1)} %relay_out.1), calls=%async_computation.3 | async-start | bytes 6291456 | tf_op jit(solution)/shard_map/all_to_all | solution.py:566
  217.1 15.4 %collective-permute-start.9 = (bf16[6,128,256]{2,1,0:T(8,128)(2,1)S(1)}, bf16[6,128,256]{2,1,0:T(8,128)(2,1)S(1)}, u32[]{:S(2)}, u32[]{:S(2)}) collective-permute-start(bf16[6,128,256]{2,1,0:T(8,128)(2,1)S(1)} %copy-done.16), channel_id=1, source_target_pairs={{2,0},{3,1},{4,2},{5,3},{6,4},{7,5},{10,8},{11,9},{12,10},{13,11},... | collective-permute-start | bytes 1179656 | tf_op jit(solution)/shard_map/ppermute | solution.py:624
  232.5 0.7 copy-start.1
  236.2 27.9 %collective-permute-start.10 = (bf16[128,768]{1,0:T(8,128)(2,1)}, bf16[128,768]{1,0:T(8,128)(2,1)S(1)}, u32[]{:S(2)}, u32[]{:S(2)}) collective-permute-start(bf16[128,768]{1,0:T(8,128)(2,1)} %get-tuple-element.51), channel_id=1, source_target_pairs={{0,0},{1,1},{2,8},{3,9},{4,16},{5,17},{6,24},{7,25},{8,2},{9,3},{1... | collective-permute-start | bytes 589832 | tf_op jit(solution)/shard_map/ppermute | solution.py:576
  242.3 26.6 %collective-permute-start.11 = (bf16[128,768]{1,0:T(8,128)(2,1)}, bf16[128,768]{1,0:T(8,128)(2,1)S(1)}, u32[]{:S(2)}, u32[]{:S(2)}) collective-permute-start(bf16[128,768]{1,0:T(8,128)(2,1)} %get-tuple-element.52), channel_id=1, source_target_pairs={{0,1},{1,0},{2,9},{3,8},{4,17},{5,16},{6,25},{7,24},{8,3},{9,2},{1... | collective-permute-start | bytes 589832 | tf_op jit(solution)/shard_map/ppermute | solution.py:576
  243.3 29.3 %collective-permute-start.12 = (bf16[128,768]{1,0:T(8,128)(2,1)}, bf16[128,768]{1,0:T(8,128)(2,1)S(1)}, u32[]{:S(2)}, u32[]{:S(2)}) collective-permute-start(bf16[128,768]{1,0:T(8,128)(2,1)} %get-tuple-element.53), channel_id=1, source_target_pairs={{0,2},{1,3},{2,10},{3,11},{4,18},{5,19},{6,26},{7,27},{8,0},{9,1},... | collective-permute-start | bytes 589832 | tf_op jit(solution)/shard_map/ppermute | solution.py:576
  246.8 31.0 %collective-permute-start.13 = (bf16[128,768]{1,0:T(8,128)(2,1)}, bf16[128,768]{1,0:T(8,128)(2,1)S(1)}, u32[]{:S(2)}, u32[]{:S(2)}) collective-permute-start(bf16[128,768]{1,0:T(8,128)(2,1)} %get-tuple-element.54), channel_id=1, source_target_pairs={{0,3},{1,2},{2,11},{3,10},{4,19},{5,18},{6,27},{7,26},{8,1},{9,0},... | collective-permute-start | bytes 589832 | tf_op jit(solution)/shard_map/ppermute | solution.py:576
  247.0 30.8 %collective-permute-start.14 = (bf16[128,768]{1,0:T(8,128)(2,1)}, bf16[128,768]{1,0:T(8,128)(2,1)S(1)}, u32[]{:S(2)}, u32[]{:S(2)}) collective-permute-start(bf16[128,768]{1,0:T(8,128)(2,1)} %get-tuple-element.55), channel_id=1, source_target_pairs={{0,4},{1,5},{2,12},{3,13},{4,20},{5,21},{6,28},{7,29},{8,6},{9,7},... | collective-permute-start | bytes 589832 | tf_op jit(solution)/shard_map/ppermute | solution.py:576
  264.1 11.3 %copy-start.5 = (bf16[128,768]{1,0:T(8,128)(2,1)}, bf16[128,768]{1,0:T(8,128)(2,1)S(1)}, u32[]{:S(2)}) copy-start(bf16[128,768]{1,0:T(8,128)(2,1)S(1)} %collective-permute-done.10.refs_2_) | copy-start | bytes 589828
  264.1 19.6 %collective-permute-start.15 = (bf16[128,768]{1,0:T(8,128)(2,1)}, bf16[128,768]{1,0:T(8,128)(2,1)S(1)}, u32[]{:S(2)}, u32[]{:S(2)}) collective-permute-start(bf16[128,768]{1,0:T(8,128)(2,1)} %get-tuple-element.56), channel_id=1, source_target_pairs={{0,5},{1,4},{2,13},{3,12},{4,21},{5,20},{6,29},{7,28},{8,7},{9,6},... | collective-permute-start | bytes 589832 | tf_op jit(solution)/shard_map/ppermute | solution.py:576
  268.9 6.5 %copy-start.6 = (bf16[128,768]{1,0:T(8,128)(2,1)}, bf16[128,768]{1,0:T(8,128)(2,1)S(1)}, u32[]{:S(2)}) copy-start(bf16[128,768]{1,0:T(8,128)(2,1)S(1)} %collective-permute-done.11.refs_3_) | copy-start | bytes 589828
  268.9 18.2 %collective-permute-start.16 = (bf16[128,768]{1,0:T(8,128)(2,1)}, bf16[128,768]{1,0:T(8,128)(2,1)S(1)}, u32[]{:S(2)}, u32[]{:S(2)}) collective-permute-start(bf16[128,768]{1,0:T(8,128)(2,1)} %get-tuple-element.57), channel_id=1, source_target_pairs={{0,6},{1,7},{2,14},{3,15},{4,22},{5,23},{6,30},{7,31},{8,4},{9,5},... | collective-permute-start | bytes 589832 | tf_op jit(solution)/shard_map/ppermute | solution.py:576
  272.6 2.8 copy-start.7
  272.6 19.7 %collective-permute-start.17 = (bf16[128,768]{1,0:T(8,128)(2,1)}, bf16[128,768]{1,0:T(8,128)(2,1)S(1)}, u32[]{:S(2)}, u32[]{:S(2)}) collective-permute-start(bf16[128,768]{1,0:T(8,128)(2,1)} %get-tuple-element.58), channel_id=1, source_target_pairs={{0,7},{1,6},{2,15},{3,14},{4,23},{5,22},{6,31},{7,30},{8,5},{9,4},... | collective-permute-start | bytes 589832 | tf_op jit(solution)/shard_map/ppermute | solution.py:576
  277.8 14.4 %copy-start.8 = (bf16[128,768]{1,0:T(8,128)(2,1)}, bf16[128,768]{1,0:T(8,128)(2,1)S(1)}, u32[]{:S(2)}) copy-start(bf16[128,768]{1,0:T(8,128)(2,1)S(1)} %collective-permute-done.13.refs_5_) | copy-start | bytes 589828
  277.8 14.4 %copy-start.9 = (bf16[128,768]{1,0:T(8,128)(2,1)}, bf16[128,768]{1,0:T(8,128)(2,1)S(1)}, u32[]{:S(2)}) copy-start(bf16[128,768]{1,0:T(8,128)(2,1)S(1)} %collective-permute-done.14.refs_6_) | copy-start | bytes 589828
  283.7 8.6 %copy-start.10 = (bf16[128,768]{1,0:T(8,128)(2,1)}, bf16[128,768]{1,0:T(8,128)(2,1)S(1)}, u32[]{:S(2)}) copy-start(bf16[128,768]{1,0:T(8,128)(2,1)S(1)} %collective-permute-done.15.refs_7_) | copy-start | bytes 589828
  287.0 5.2 %copy-start.11 = (bf16[128,768]{1,0:T(8,128)(2,1)}, bf16[128,768]{1,0:T(8,128)(2,1)S(1)}, u32[]{:S(2)}) copy-start(bf16[128,768]{1,0:T(8,128)(2,1)S(1)} %collective-permute-done.16.refs_8_) | copy-start | bytes 589828
  (2 other events, 1.4 us)
where the time goes:
time: 297 us
  waiting for transfers between devices  174 us (59%)
  Pallas kernels  60 us (20%)
  starting transfers between devices  56.8 us (19%)
  local copies, waits for them, and re-layouts  4.61 us (2%)
    ppermute x9, waiting for transfers between devices, along(): lax.ppermute(x, axes, [(device(a, b, c), device(a, b ^ k, c)) for a, b, c...  75.3 us
    all_to_all x5, waiting for transfers between devices, swap(): lax.all_to_all(x, plane_axes, split_axis=0, concat_axis=0, tiled=True)  51.3 us
    ppermute x8, waiting for transfers between devices, home(): return lax.ppermute(x, axes, pairs)  38.9 us
    pallas_call x2, Pallas kernels, attend(): pl.pallas_call(kernel, in_specs=[pl.BlockSpec(memory_space=pltpu.SMEM)] +...  36.3 us
    all_to_all x5, starting transfers between devices, swap(): lax.all_to_all(x, plane_axes, split_axis=0, concat_axis=0, tiled=True)  27.7 us
    ppermute x8, starting transfers between devices, home(): return lax.ppermute(x, axes, pairs)  12.3 us
    ppermute x9, starting transfers between devices, along(): lax.ppermute(x, axes, [(device(a, b, c), device(a, b ^ k, c)) for a, b, c...  9.76 us
    ppermute x1, waiting for transfers between devices, body(): back = lax.ppermute(back, axes, down)  8.31 us
  transfers between devices with their start and end apart: 23, of which 15 were waited for; matrix products, arithmetic and copies ran while one was open for 0% of the time, Pallas kernels for 18%

commit v1 on v0

--- a/solution.py
+++ b/solution.py
@@ -70,10 +70,10 @@
 
 
 def pack_first(query_rows, key_rows, value_rows, groups):
-    width = QH // groups * DH
+    half = QH // groups * DH // CHUNKS
     repeats = groups // KVH
     sources = [
-        (query_rows, width, lambda r: r),
+        (query_rows, half, lambda r: r * CHUNKS),
         (key_rows, DH, lambda r: r // repeats),
         (value_rows, DH, lambda r: r // repeats),
     ]
@@ -85,56 +85,90 @@
     return pack([(rows, half, lambda r: r * CHUNKS + chunk)], groups)
 
 
+def pack_grad(core_index, rows, chunk, groups):
+    count = rows.shape[0]
+    half = QH // groups * DH // CHUNKS
+
+    def kernel(core_ref, in_ref, *refs):
+        outs, (held, sem_in, sem_out) = refs[:groups], refs[groups:]
+        loads, stores = [], []
+        for k in range(groups):
+            col = pl.multiple_of(((core_ref[0] ^ k) * CHUNKS + chunk) * half, half)
+            copy = pltpu.make_async_copy(in_ref.at[:, pl.ds(col, half)], held.at[k], sem_in.at[k])
+            copy.start()
+            loads.append(copy)
+        for k in range(groups):
+            loads[k].wait()
+            copy = pltpu.make_async_copy(held.at[k], outs[k], sem_out.at[k])
+            copy.start()
+            stores.append(copy)
+        for copy in stores:
+            copy.wait()
+
+    return list(
+        pl.pallas_call(
+            kernel,
+            in_specs=[pl.BlockSpec(memory_space=pltpu.SMEM), ANY],
+            out_specs=[ANY] * groups,
+            out_shape=[jax.ShapeDtypeStruct((count, half), BF16)] * groups,
+            scratch_shapes=[
+                pltpu.VMEM((groups, count, half), BF16),
+                pltpu.SemaphoreType.DMA((groups,)),
+                pltpu.SemaphoreType.DMA((groups,)),
+            ],
+            cost_estimate=pl.CostEstimate(
+                flops=0, bytes_accessed=4 * groups * count * half, transcendentals=0
+            ),
+            compiler_params=pltpu.CompilerParams(vmem_limit_bytes=62 << 20),
+            name="pack_grad",
+        )(core_index, rows)
+    )
+
+
 def relay_in(plane_index, arrived, width):
-    n_plane, per_plane = arrived.shape[:2]
-    kv = 2 * DH
+    n_plane, per_plane, _, total = arrived.shape
+    halo = total - width
+    form = (per_plane, BLOCK, total + halo)
+    copies = 2 if halo else 1
 
     def kernel(plane_ref, in_ref, *refs):
-        firsts, refs = refs[:n_plane], refs[n_plane:]
-        seconds, (one, two, sem_in, sem_out) = refs[:n_plane], refs[n_plane:]
+        outs, (held, sem_in, sem_out) = refs[:n_plane], refs[n_plane:]
         loads, stores = [], []
         for k in range(n_plane):
             to = plane_ref[0] ^ k
-            near = jnp.maximum(to - 1, 0)
-            views = [
-                (in_ref.at[to, :, :, :width], one.at[k, :, :, :width]),
-                (in_ref.at[to, :, :, 2 * width :], one.at[k, :, :, width : width + kv]),
-                (in_ref.at[near, :, :, 2 * width :], one.at[k, :, :, width + kv :]),
-                (in_ref.at[to, :, :, width : 2 * width], two.at[k]),
-            ]
+            views = [(in_ref.at[to], held.at[k, :, :, :total] if halo else held.at[k])]
+            if halo:
+                near = jnp.maximum(to - 1, 0)
+                views.append((in_ref.at[near, :, :, width:], held.at[k, :, :, total:]))
             for n, (src, dst) in enumerate(views):
-                copy = pltpu.make_async_copy(src, dst, sem_in.at[4 * k + n])
+                copy = pltpu.make_async_copy(src, dst, sem_in.at[copies * k + n])
                 copy.start()
                 loads.append(copy)
         for k in range(n_plane):
-            for copy in loads[4 * k : 4 * k + 4]:
+            for copy in loads[copies * k : copies * (k + 1)]:
                 copy.wait()
-            for n, (src, dst) in enumerate(((one.at[k], firsts[k]), (two.at[k], seconds[k]))):
-                copy = pltpu.make_async_copy(src, dst, sem_out.at[2 * k + n])
-                copy.start()
-                stores.append(copy)
-        for copy in stores:
-            copy.wait()
-
-    one = (per_plane, BLOCK, width + 2 * kv)
-    two = (per_plane, BLOCK, width)
-    results = pl.pallas_call(
-        kernel,
-        in_specs=[pl.BlockSpec(memory_space=pltpu.SMEM), ANY],
-        out_specs=[ANY] * (2 * n_plane),
-        out_shape=[jax.ShapeDtypeStruct(one, BF16)] * n_plane
-        + [jax.ShapeDtypeStruct(two, BF16)] * n_plane,
-        scratch_shapes=[
-            pltpu.VMEM((n_plane, *one), BF16),
-            pltpu.VMEM((n_plane, *two), BF16),
-            pltpu.SemaphoreType.DMA((4 * n_plane,)),
-            pltpu.SemaphoreType.DMA((2 * n_plane,)),
-        ],
-        cost_estimate=pl.CostEstimate(flops=0, bytes_accessed=6 << 20, transcendentals=0),
-        compiler_params=pltpu.CompilerParams(vmem_limit_bytes=62 << 20),
-        name="relay_in",
-    )(plane_index, arrived)
-    return list(results[:n_plane]), list(results[n_plane:])
+            copy = pltpu.make_async_copy(held.at[k], outs[k], sem_out.at[k])
+            copy.start()
+            stores.append(copy)
+        for copy in stores:
+            copy.wait()
+
+    return list(
+        pl.pallas_call(
+            kernel,
+            in_specs=[pl.BlockSpec(memory_space=pltpu.SMEM), ANY],
+            out_specs=[ANY] * n_plane,
+            out_shape=[jax.ShapeDtypeStruct(form, BF16)] * n_plane,
+            scratch_shapes=[
+                pltpu.VMEM((n_plane, *form), BF16),
+                pltpu.SemaphoreType.DMA((copies * n_plane,)),
+                pltpu.SemaphoreType.DMA((n_plane,)),
+            ],
+            cost_estimate=pl.CostEstimate(flops=0, bytes_accessed=4 << 20, transcendentals=0),
+            compiler_params=pltpu.CompilerParams(vmem_limit_bytes=62 << 20),
+            name="relay_in",
+        )(plane_index, arrived)
+    )
 
 
 def relay_out(plane_index, parts, held):
@@ -177,16 +211,16 @@
     )(plane_index, *parts, held)
 
 
-def attend(table, kv_parts, query_parts, grad_slots, carried, last, shard_blocks, out_form):
+def attend(table, kv_parts, query_parts, grad_parts, carried, last, shard_blocks, out_form):
     n_src = len(kv_parts)
     per_src = kv_parts[0].shape[0]
     blocks = shard_blocks
-    width = grad_slots.shape[-1]
-    slots = grad_slots.shape[0]
-    per_core = slots // out_form[0]
+    width = grad_parts[0].shape[-1]
+    per_core = grad_parts[0].shape[0] // BLOCK
+    slots = per_core * len(grad_parts)
+    owner = 2 * blocks + 2
     base = blocks - HALO
     span = blocks + HALO
-    pairs = width // (2 * DH)
     scale = 1.0 / math.sqrt(DH)
     exponent = scale * math.log2(math.e)
     first = carried is None
@@ -196,7 +230,7 @@
         tab = refs.pop(0)
         kv_refs = [refs.pop(0) for _ in range(n_src)]
         q_refs = kv_refs if first else [refs.pop(0) for _ in range(n_src)]
-        go_ref = refs.pop(0)
+        go_refs = [refs.pop(0) for _ in grad_parts]
         carried_ref = None if first else refs.pop(0)
         out_ref = refs.pop(0)
         if last:
@@ -229,19 +263,24 @@
             row = pl.multiple_of(slot % per_core * BLOCK, BLOCK)
             return out_ref.at[slot // per_core, pl.ds(row, BLOCK), :]
 
-        def go_copy(i):
-            return pltpu.make_async_copy(go_ref.at[tab[i]], gs.at[i], sem_go.at[i])
+        def go_copy(k, at, i):
+            rows = go_refs[k].at[at * BLOCK : (at + 1) * BLOCK, :]
+            return pltpu.make_async_copy(rows, gs.at[i], sem_go.at[i])
 
         def out_copy(i):
             return pltpu.make_async_copy(os.at[i], slot_ref(tab[i]), sem_out.at[i])
 
-        @pl.loop(0, blocks)
-        def _(i):
-            go_copy(i).start()
+        for k in range(len(grad_parts)):
+            for at in range(per_core):
+                i = tab[owner + (core ^ k) * per_core + at]
+
+                @pl.when(i < blocks)
+                def _():
+                    go_copy(k, at, i).start()
 
         zero[...] = jnp.zeros_like(zero)
         for slot in range(slots):
-            @pl.when(tab[2 * blocks + 2 + slot] == 0)
+            @pl.when(tab[owner + slot] >= blocks)
             def _():
                 pltpu.make_async_copy(zero, slot_ref(slot), sem_end.at[slot]).start()
 
@@ -256,8 +295,8 @@
             kts[:, pl.ds(at, DH)] = kvs[base + b, :, :DH].T
             vts[:, pl.ds(at, DH)] = kvs[base + b, :, DH:].T
 
-        key_at = lax.broadcasted_iota(jnp.int32, (BLOCK, 2 * BLOCK), 0)
-        query_at = lax.broadcasted_iota(jnp.int32, (BLOCK, 2 * BLOCK), 1) % BLOCK
+        key_at = lax.broadcasted_iota(jnp.int32, (BLOCK, width), 0)
+        query_at = lax.broadcasted_iota(jnp.int32, (BLOCK, width), 1) % BLOCK
         causal = key_at <= query_at
 
         def block_body(n, i, k):
@@ -269,35 +308,33 @@
             lane = pl.multiple_of(rel * DH, DH)
             keys_t = kts[:, pl.ds(lane, size)]
             values_t = vts[:, pl.ds(lane, size)]
-            for pair in range(pairs):
-                c0 = pair * 2 * DH
-                q2 = jnp.concatenate([qs[i, :, c0 : c0 + DH], qs[i, :, c0 + DH : c0 + 2 * DH]], axis=0)
-                g2 = jnp.concatenate([gs[i, :, c0 : c0 + DH], gs[i, :, c0 + DH : c0 + 2 * DH]], axis=0)
-                s = lax.dot_general(keys, q2, NT, preferred_element_type=F32)
-                diag = jnp.where(causal, s[size - BLOCK :], -jnp.inf)
-                s = jnp.concatenate([s[: size - BLOCK], diag], axis=0) if n > 1 else diag
-                top = jnp.max(s, axis=0, keepdims=True)
-                p = jnp.exp2((s - top) * exponent)
-                w = p * (1.0 / jnp.sum(p, axis=0, keepdims=True))
-                wb = w.astype(BF16)
-                o_t = jnp.dot(values_t, wb, preferred_element_type=F32)
-                dp = lax.dot_general(values, g2, NT, preferred_element_type=F32)
-                delta = jnp.sum(w * dp, axis=0, keepdims=True)
-                ds = (w * (dp - delta)).astype(BF16)
-                dq_t = jnp.dot(keys_t, ds, preferred_element_type=F32) * scale
-                dk = jnp.dot(ds, q2, preferred_element_type=F32)
-                dv = jnp.dot(wb, g2, preferred_element_type=F32)
-                acc[pl.ds(rel, n), :, :DH] += dk.reshape(n, BLOCK, DH)
-                acc[pl.ds(rel, n), :, DH:] += dv.reshape(n, BLOCK, DH)
-                for side in range(2):
-                    c1 = c0 + side * DH
-                    os[i, :, c1 : c1 + DH] = o_t[:, side * BLOCK : (side + 1) * BLOCK].T.astype(BF16)
-                    gqs[k, :, c1 : c1 + DH] = dq_t[:, side * BLOCK : (side + 1) * BLOCK].T.astype(BF16)
+            cols = [slice(c, c + DH) for c in range(0, width, DH)]
+            q_all = jnp.concatenate([qs[i, :, c] for c in cols], axis=0)
+            g_all = jnp.concatenate([gs[i, :, c] for c in cols], axis=0)
+            s = lax.dot_general(keys, q_all, NT, preferred_element_type=F32)
+            dp = lax.dot_general(values, g_all, NT, preferred_element_type=F32)
+            diag = jnp.where(causal, s[size - BLOCK :], -jnp.inf)
+            s = jnp.concatenate([s[: size - BLOCK], diag], axis=0) if n > 1 else diag
+            top = jnp.max(s, axis=0, keepdims=True)
+            p = jnp.exp2((s - top) * exponent)
+            w = p * (1.0 / jnp.sum(p, axis=0, keepdims=True))
+            wb = w.astype(BF16)
+            delta = jnp.sum(w * dp, axis=0, keepdims=True)
+            ds = (w * (dp - delta)).astype(BF16)
+            o_t = jnp.dot(values_t, wb, preferred_element_type=F32)
+            dq_t = jnp.dot(keys_t, ds, preferred_element_type=F32) * scale
+            dk = jnp.dot(ds, q_all, preferred_element_type=F32)
+            dv = jnp.dot(wb, g_all, preferred_element_type=F32)
+            acc[pl.ds(rel, n), :, :DH] += dk.reshape(n, BLOCK, DH)
+            acc[pl.ds(rel, n), :, DH:] += dv.reshape(n, BLOCK, DH)
+            for c in cols:
+                os[i, :, c] = o_t[:, c].T.astype(BF16)
+                gqs[k, :, c] = dq_t[:, c].T.astype(BF16)
 
         @pl.loop(0, blocks)
         def _(k):
             i = core ^ k
-            go_copy(i).wait()
+            go_copy(0, 0, i).wait()
             count = tab[blocks + i]
             at = k if last else ((i // per_src) ^ plane) * per_src + i % per_src
             for n in range(1, DOCMAX + 1):
@@ -336,14 +373,14 @@
             out_copy(i).wait()
 
         for slot in range(slots):
-            @pl.when(tab[2 * blocks + 2 + slot] == 0)
+            @pl.when(tab[owner + slot] >= blocks)
             def _():
                 pltpu.make_async_copy(zero, slot_ref(slot), sem_end.at[slot]).wait()
 
     operands = [table, *kv_parts]
     if not first:
         operands += query_parts
-    operands.append(grad_slots)
+    operands += grad_parts
     if not first:
         operands.append(carried)
     out_shape = [jax.ShapeDtypeStruct((*out_form, width), BF16)]
@@ -438,14 +475,13 @@
     )(core_index, rows, main, back)
 
 
-def place_rows(block_index, arrived, last_rows, groups):
+def place_rows(block_index, last_rows, groups):
     repeats = groups // KVH
     width = QH // groups * DH
     half = width // CHUNKS
-    first_row = arrived.shape[1] - BLOCK
 
     def kernel(*refs):
-        at_ref, arrived_ref, *refs = refs
+        at_ref, *refs = refs
         lasts, refs = refs[:groups], refs[groups:]
         gq_ref, gk_ref, gv_ref, rows, held, sums, sem_in, sem_out = refs
         at = at_ref[0]
@@ -461,16 +497,15 @@
             copy.start()
             stores.append(copy)
 
-        for r in range(groups):
-            load(arrived_ref.at[r, first_row:, :], rows.at[:, r * width : r * width + half])
         for k in range(groups):
-            group = at ^ k
-            col = pl.multiple_of(group * width + half, half)
-            load(lasts[k].at[:, :half], rows.at[:, pl.ds(col, half)])
-            load(lasts[k].at[:, half:], held.at[group])
-        for copy in loads:
-            copy.wait()
-        store(rows, gq_ref)
+            load(lasts[k].at[:, :half], rows.at[k])
+            load(lasts[k].at[:, half:], held.at[at ^ k])
+        for k in range(groups):
+            col = pl.multiple_of((at ^ k) * width + half, half)
+            loads[2 * k].wait()
+            store(rows.at[k], gq_ref.at[:, pl.ds(col, half)])
+        for k in range(groups):
+            loads[2 * k + 1].wait()
         for head in range(KVH):
             total = held[head * repeats].astype(F32)
             for extra in range(1, repeats):
@@ -484,7 +519,7 @@
 
     return pl.pallas_call(
         kernel,
-        in_specs=[pl.BlockSpec(memory_space=pltpu.SMEM)] + [ANY] * (groups + 1),
+        in_specs=[pl.BlockSpec(memory_space=pltpu.SMEM)] + [ANY] * groups,
         out_specs=[ANY] * 3,
         out_shape=[
             jax.ShapeDtypeStruct((BLOCK, QH * DH), BF16),
@@ -492,32 +527,71 @@
             jax.ShapeDtypeStruct((BLOCK, KVH * DH), BF16),
         ],
         scratch_shapes=[
-            pltpu.VMEM((BLOCK, QH * DH), BF16),
+            pltpu.VMEM((groups, BLOCK, half), BF16),
             pltpu.VMEM((groups, BLOCK, 2 * DH), BF16),
             pltpu.VMEM((2, BLOCK, KVH * DH), BF16),
-            pltpu.SemaphoreType.DMA((3 * groups,)),
-            pltpu.SemaphoreType.DMA((3,)),
+            pltpu.SemaphoreType.DMA((2 * groups,)),
+            pltpu.SemaphoreType.DMA((groups + 2,)),
         ],
+        cost_estimate=pl.CostEstimate(flops=0, bytes_accessed=4 << 20, transcendentals=0),
+        compiler_params=pltpu.CompilerParams(vmem_limit_bytes=62 << 20),
+        name="place_rows",
+    )(block_index, *last_rows)
+
+
+def place_last(parts, out, grad_query):
+    groups, total, half = parts.shape
+    rows = total - BLOCK
+
+    def kernel(in_ref, _, __, out_ref, gq_ref, buf, sem_in, sem_out):
+        loads = [pltpu.make_async_copy(in_ref.at[r], buf.at[r], sem_in.at[r]) for r in range(groups)]
+        stores = []
+        for copy in loads:
+            copy.start()
+        for r in range(groups):
+            first, second = 2 * r * half, (2 * r + 1) * half
+            loads[r].wait()
+            pairs = [
+                (buf.at[r, :rows, :], out_ref.at[:, second : second + half]),
+                (buf.at[r, rows:, :], gq_ref.at[:, first : first + half]),
+            ]
+            for n, (src, dst) in enumerate(pairs):
+                copy = pltpu.make_async_copy(src, dst, sem_out.at[2 * r + n])
+                copy.start()
+                stores.append(copy)
+        for copy in stores:
+            copy.wait()
+
+    return pl.pallas_call(
+        kernel,
+        in_specs=[ANY] * 3,
+        out_specs=[ANY] * 2,
+        out_shape=[
+            jax.ShapeDtypeStruct(out.shape, BF16),
+            jax.ShapeDtypeStruct(grad_query.shape, BF16),
+        ],
+        scratch_shapes=[
+            pltpu.VMEM((groups, total, half), BF16),
+            pltpu.SemaphoreType.DMA((groups,)),
+            pltpu.SemaphoreType.DMA((2 * groups,)),
+        ],
+        input_output_aliases={1: 0, 2: 1},
         cost_estimate=pl.CostEstimate(flops=0, bytes_accessed=6 << 20, transcendentals=0),
         compiler_params=pltpu.CompilerParams(vmem_limit_bytes=62 << 20),
-        name="place_rows",
-    )(block_index, arrived, *last_rows)
-
-
-def place_out(parts, rows, chunk, held):
-    groups, _, half = parts.shape
-
-    def kernel(*refs):
-        in_ref, (out_ref, buf, sem_in, sem_out) = refs[0], refs[-4:]
-        loads = [
-            pltpu.make_async_copy(in_ref.at[r, :rows, :], buf.at[r], sem_in.at[r])
-            for r in range(groups)
-        ]
+        name="place_last",
+    )(parts, out, grad_query)
+
+
+def place_out(parts):
+    groups, rows, half = parts.shape
+
+    def kernel(in_ref, out_ref, buf, sem_in, sem_out):
+        loads = [pltpu.make_async_copy(in_ref.at[r], buf.at[r], sem_in.at[r]) for r in range(groups)]
         stores = []
         for copy in loads:
             copy.start()
         for r in range(groups):
-            col = (r * CHUNKS + chunk) * half
+            col = CHUNKS * r * half
             loads[r].wait()
             copy = pltpu.make_async_copy(buf.at[r], out_ref.at[:, col : col + half], sem_out.at[r])
             copy.start()
@@ -525,10 +599,9 @@
         for copy in stores:
             copy.wait()
 
-    operands = [parts] if held is None else [parts, held]
     return pl.pallas_call(
         kernel,
-        in_specs=[ANY] * len(operands),
+        in_specs=[ANY],
         out_specs=ANY,
         out_shape=jax.ShapeDtypeStruct((rows, QH * DH), BF16),
         scratch_shapes=[
@@ -536,13 +609,12 @@
             pltpu.SemaphoreType.DMA((groups,)),
             pltpu.SemaphoreType.DMA((groups,)),
         ],
-        input_output_aliases={} if held is None else {1: 0},
         cost_estimate=pl.CostEstimate(
             flops=0, bytes_accessed=4 * groups * rows * half, transcendentals=0
         ),
         compiler_params=pltpu.CompilerParams(vmem_limit_bytes=62 << 20),
         name="place_out",
-    )(*operands)
+    )(parts)
 
 
 def body(shape, query_rows, key_rows, value_rows, grad_out, doc_ids, route_table):
@@ -584,31 +656,38 @@
     counts = sum(
         (docs[HALO - d : HALO - d + blocks] == own).astype(jnp.int32) for d in range(DOCMAX)
     )
-    live = (routes < blocks).astype(jnp.int32)
-    table = jnp.concatenate(
-        [slot_of, counts, jnp.stack([plane, core]).astype(jnp.int32), live]
-    )
+    table = jnp.concatenate([slot_of, counts, jnp.stack([plane, core]).astype(jnp.int32), routes])
 
     def spread(x):
         return x.reshape((n_seq, per_plane) + x.shape[1:])
 
-    def by_slot(x):
-        return x.reshape(slots, BLOCK, x.shape[-1])
+    def across(x, k):
+        pairs = []
+        for a, b, c in every:
+            to = (a * per_plane + c) ^ k
+            pairs.append((device(a, b, c), device(to // per_plane, b, to % per_plane)))
+        return lax.ppermute(x, axes, pairs)
 
     first_pack = pack_first(query_rows, key_rows, value_rows, groups)
     first_plane = spread(swap(first_pack))
-    grad_pack = pack_half(grad_out, 0, groups)
-    grad_pack_second = pack_half(grad_out, 1, groups)
-    width = grad_pack.shape[-1]
+    core_index = core.astype(jnp.int32).reshape(1)
+    grad_first = pack_grad(core_index, grad_out, 0, groups)
+    second_pack = pack_half(query_rows, 1, groups)
+    grad_second = pack_grad(core_index, grad_out, 1, groups)
+    width = second_pack.shape[-1]
 
     plane_index = plane.astype(jnp.int32).reshape(1)
-    kv_parts, query_parts = relay_in(plane_index, first_plane, width)
+    kv_parts = relay_in(plane_index, first_plane, width)
     for k in range(1, n_plane):
         kv_parts[k] = along(kv_parts[k], k)
+    second_plane = spread(swap(second_pack))
+    query_parts = relay_in(plane_index, second_plane, width)
     for k in range(1, n_plane):
         query_parts[k] = along(query_parts[k], k)
-    grad_first = by_slot(swap(grad_pack))
-    grad_second = by_slot(swap(grad_pack_second))
+    for k in range(1, groups):
+        grad_first[k] = across(grad_first[k], k)
+    for k in range(1, groups):
+        grad_second[k] = across(grad_second[k], k)
 
     rows = grad_out.shape[0]
     out_first, *rows_first, carried = attend(
@@ -624,17 +703,15 @@
     back = lax.ppermute(back, axes, down)
     out_second = relay_out(plane_index, rows_first, out_second)
     back_second = swap(out_second)
-    rows_second = finish(core.astype(jnp.int32).reshape(1), rows_second, main, back)
+    rows_second = finish(core_index, rows_second, main, back)
     home_second = []
     for k in range(blocks):
         home_second.append(home(rows_second[k], k))
 
-    attn_out = place_out(back_first, rows, 0, None)
+    attn_out = place_out(back_first)
     block_index = (plane * per_plane + part).astype(jnp.int32).reshape(1)
-    grad_query, grad_key, grad_value = place_rows(
-        block_index, back_second, home_second, groups
-    )
-    attn_out = place_out(back_second, rows, 1, attn_out)
+    grad_query, grad_key, grad_value = place_rows(block_index, home_second, groups)
+    attn_out, grad_query = place_last(back_second, attn_out, grad_query)
     return (attn_out, grad_query, grad_key, grad_value)
 
 

time: 297 us -> 286 us (0.963)
  waiting for transfers between devices: 174 us -> 161 us
  starting transfers between devices: 56.8 us -> 64.9 us
  Pallas kernels: 60 us -> 53.7 us
    ppermute x0 -> x14, waiting for transfers between devices: none -> 62.4 us  [across(): return lax.ppermute(x, axes, pairs)]
    ppermute x9, waiting for transfers between devices: 75.3 us -> 33.9 us  [along(): lax.ppermute(x, axes, [(device(a, b, c), device(a, b ^ k, c)) for a, b, c...]
    all_to_all x5 -> x4, waiting for transfers between devices: 51.3 us -> 13.4 us  [swap(): lax.all_to_all(x, plane_axes, split_axis=0, concat_axis=0, tiled=True)]
    ppermute x0 -> x14, starting transfers between devices: none -> 14.6 us  [across(): return lax.ppermute(x, axes, pairs)]
    pallas_call x2, Pallas kernels: 36.3 us -> 27 us  [attend(): pl.pallas_call(kernel, in_specs=[pl.BlockSpec(memory_space=pltpu.SMEM)] +...]
    all_to_all x5 -> x4, starting transfers between devices: 27.7 us -> 19.8 us  [swap(): lax.all_to_all(x, plane_axes, split_axis=0, concat_axis=0, tiled=True)]
    pallas_call x2 -> x4, Pallas kernels: 4.79 us -> 10.2 us  [the longest x2 4.92 us: pack_grad(): pl.pallas_call(kernel, in_specs=[pl.BlockSpec(memory_space=pltpu.SMEM), A...]
    ppermute x8, waiting for transfers between devices: 38.9 us -> 42.5 us  [home(): return lax.ppermute(x, axes, pairs)]
  transfers between devices with their start and end apart: 23 -> 36, of which waited for: 15 -> 19; matrix products, arithmetic and copies ran while one was open for 0% -> 0% of each run, Pallas kernels for 18% -> 17%
where the time goes in v1:
time: 286 us; the launch traced here: 285 us
  waiting for transfers between devices  161 us (56%)
  starting transfers between devices  64.9 us (23%)
  Pallas kernels  53.7 us (19%)
  local copies, waits for them, and re-layouts  4.59 us (2%)
    ppermute x14, waiting for transfers between devices, across(): return lax.ppermute(x, axes, pairs)  62.4 us
    ppermute x8, waiting for transfers between devices, home(): return lax.ppermute(x, axes, pairs)  42.5 us
    ppermute x9, waiting for transfers between devices, along(): lax.ppermute(x, axes, [(device(a, b, c), device(a, b ^ k, c)) for a, b, c...  33.9 us
    pallas_call x2, Pallas kernels, attend(): pl.pallas_call(kernel, in_specs=[pl.BlockSpec(memory_space=pltpu.SMEM)] +...  27 us
    all_to_all x4, starting transfers between devices, swap(): lax.all_to_all(x, plane_axes, split_axis=0, concat_axis=0, tiled=True)  19.8 us
    ppermute x14, starting transfers between devices, across(): return lax.ppermute(x, axes, pairs)  14.6 us
    all_to_all x4, waiting for transfers between devices, swap(): lax.all_to_all(x, plane_axes, split_axis=0, concat_axis=0, tiled=True)  13.4 us
    ppermute x8, starting transfers between devices, home(): return lax.ppermute(x, axes, pairs)  13.3 us
  transfers between devices with their start and end apart: 36, of which 19 were waited for; matrix products, arithmetic and copies ran while one was open for 0% of the time, Pallas kernels for 17%

profile of v1, /device:TPU:17, one launch (start us, length us, event | category | flops | bytes accessed | tf_op | source)
XLA Modules:
  0.0 285.1 jit_solution(6641684015605243611)
XLA Ops:
  0.6 2.4 shard_map.93
  3.1 4.4 %all-to-all-start = ((bf16[8,128,768]{2,1,0:T(8,128)(2,1)}), bf16[8,128,768]{2,1,0:T(8,128)(2,1)S(1)}, u32[]{:S(2)}, u32[]{:S(2)}) async-start(bf16[8,128,768]{2,1,0:T(8,128)(2,1)} %shard_map.93), calls=%async_computation | async-start | bytes 3145728 | tf_op jit(solution)/shard_map/all_to_all | solution.py:638
  7.5 2.4 pack_grad.2
  9.9 1.4 collective-permute-start.3
  12.0 2.1 shard_map.94
  14.1 13.4 %all-to-all-done = bf16[8,128,768]{2,1,0:T(8,128)(2,1)S(1)} async-done(((bf16[8,128,768]{2,1,0:T(8,128)(2,1)}), bf16[8,128,768]{2,1,0:T(8,128)(2,1)S(1)}, u32[]{:S(2)}, u32[]{:S(2)}) %all-to-all-start) | async-done | bytes 1572896 | tf_op jit(solution)/shard_map/all_to_all | solution.py:638
  27.5 4.5 %all-to-all-start.1 = ((bf16[8,128,512]{2,1,0:T(8,128)(2,1)}), bf16[8,128,512]{2,1,0:T(8,128)(2,1)}, u32[]{:S(2)}, u32[]{:S(2)}) async-start(bf16[8,128,512]{2,1,0:T(8,128)(2,1)} %shard_map.94), calls=%async_computation.1 | async-start | bytes 2097152 | tf_op jit(solution)/shard_map/all_to_all | solution.py:638
  32.0 1.4 collective-permute-start.6
  34.6 2.5 relay_in.2
  40.5 16.4 %collective-permute-done.6.refs_9_ = bf16[256,512]{1,0:T(8,128)(2,1)} collective-permute-done((bf16[256,512]{1,0:T(8,128)(2,1)}, bf16[256,512]{1,0:T(8,128)(2,1)}, u32[]{:S(2)}, u32[]{:S(2)}) %collective-permute-start.6) | collective-permute-done | bytes 262176 | tf_op jit(solution)/shard_map/ppermute | solution.py:669
  57.8 1.7 collective-permute-start.9
  60.3 11.0 %collective-permute-done.8.refs_11_ = bf16[256,512]{1,0:T(8,128)(2,1)S(1)} collective-permute-done((bf16[256,512]{1,0:T(8,128)(2,1)}, bf16[256,512]{1,0:T(8,128)(2,1)S(1)}, u32[]{:S(2)}, u32[]{:S(2)}) %collective-permute-start.8) | collective-permute-done | bytes 262176 | tf_op jit(solution)/shard_map/ppermute | solution.py:669
  71.4 14.0 %collective-permute-done.2.refs_4_ = bf16[2,128,1024]{2,1,0:T(8,128)(2,1)S(1)} collective-permute-done((bf16[2,128,1024]{2,1,0:T(8,128)(2,1)}, bf16[2,128,1024]{2,1,0:T(8,128)(2,1)S(1)}, u32[]{:S(2)}, u32[]{:S(2)}) %collective-permute-start.2) | collective-permute-done | bytes 524320 | tf_op jit(solution)/shard_map/ppermute | solution.py:641
  86.1 13.2 %attend_first.1 = (bf16[8,256,512]{2,1,0:T(8,128)(2,1)}, bf16[2,128,512]{2,1,0:T(8,128)(2,1)}, bf16[2,128,512]{2,1,0:T(8,128)(2,1)}, bf16[2,128,512]{2,1,0:T(8,1...) custom-call(s32[34]{0:T(128)} %concatenate.7.refs_0_, bf16[2,128,1024]{2,1,0:T(8,128)(2,1)} %get-tuple-element.51.refs_1_, ...), custom_call_target="tpu_custom_call" | custom-call | flops 2684354560 | bytes 12582912 | tf_op jit(solution)/shard_map/attend_first/pallas_call | solution.py:414
  99.4 6.0 %all-to-all-start.3 = ((bf16[8,256,512]{2,1,0:T(8,128)(2,1)}), bf16[8,256,512]{2,1,0:T(8,128)(2,1)}, u32[]{:S(2)}, u32[]{:S(2)}) async-start(bf16[8,256,512]{2,1,0:T(8,128)(2,1)} %get-tuple-element.81), calls=%async_computation.3 | async-start | bytes 4194304 | tf_op jit(solution)/shard_map/all_to_all | solution.py:638
  105.4 2.5 pack_grad.3
  107.9 1.4 collective-permute-start.16
  110.0 1.4 collective-permute-start.19
  112.5 2.0 relay_in.3
  114.5 21.2 %collective-permute-done.16.refs_10_ = bf16[256,512]{1,0:T(8,128)(2,1)S(1)} collective-permute-done((bf16[256,512]{1,0:T(8,128)(2,1)}, bf16[256,512]{1,0:T(8,128)(2,1)S(1)}, u32[]{:S(2)}, u32[]{:S(2)}) %collective-permute-start.16) | collective-permute-done | bytes 262176 | tf_op jit(solution)/shard_map/ppermute | solution.py:669
  135.7 2.6 collective-permute-start.21
  138.4 4.0 %collective-permute-done.18.refs_12_ = bf16[256,512]{1,0:T(8,128)(2,1)S(1)} collective-permute-done((bf16[256,512]{1,0:T(8,128)(2,1)}, bf16[256,512]{1,0:T(8,128)(2,1)S(1)}, u32[]{:S(2)}, u32[]{:S(2)}) %collective-permute-start.18) | collective-permute-done | bytes 262176 | tf_op jit(solution)/shard_map/ppermute | solution.py:669
  142.5 3.1 %collective-permute-start.14 = (bf16[2,128,512]{2,1,0:T(8,128)(2,1)}, bf16[2,128,512]{2,1,0:T(8,128)(2,1)S(1)}, u32[]{:S(2)}, u32[]{:S(2)}) collective-permute-start(bf16[2,128,512]{2,1,0:T(8,128)(2,1)} %get-tuple-element.69), channel_id=1, source_target_pairs={{0,4},{1,5},{2,6},{3,7},{4,0},{5,1},{6,2},{7,3},{8,12},{9,13},{10,... | collective-permute-start | bytes 786440 | tf_op jit(solution)/shard_map/ppermute | solution.py:641
  145.6 2.4 collective-permute-done.20.refs_14_
  148.0 2.0 collective-permute-start.15
  150.0 6.9 %collective-permute-done.21.refs_15_ = bf16[256,512]{1,0:T(8,128)(2,1)S(1)} collective-permute-done((bf16[256,512]{1,0:T(8,128)(2,1)}, bf16[256,512]{1,0:T(8,128)(2,1)S(1)}, u32[]{:S(2)}, u32[]{:S(2)}) %collective-permute-start.21) | collective-permute-done | bytes 262176 | tf_op jit(solution)/shard_map/ppermute | solution.py:669
  157.0 3.1 %collective-permute-start.11 = (bf16[2,128,512]{2,1,0:T(8,128)(2,1)S(1)}, bf16[2,128,512]{2,1,0:T(8,128)(2,1)S(1)}, u32[]{:S(2)}, u32[]{:S(2)}) collective-permute-start(bf16[2,128,512]{2,1,0:T(8,128)(2,1)S(1)} %copy-done.19), channel_id=1, source_target_pairs={{0,4},{1,5},{2,6},{3,7},{4,0},{5,1},{6,2},{7,3},{8,12},{9,13},{10,... | collective-permute-start | bytes 786440 | tf_op jit(solution)/shard_map/ppermute | solution.py:641
  160.3 3.1 %collective-permute-done.14.refs_7_ = bf16[2,128,512]{2,1,0:T(8,128)(2,1)S(1)} collective-permute-done((bf16[2,128,512]{2,1,0:T(8,128)(2,1)}, bf16[2,128,512]{2,1,0:T(8,128)(2,1)S(1)}, u32[]{:S(2)}, u32[]{:S(2)}) %collective-permute-start.14) | collective-permute-done | bytes 262176 | tf_op jit(solution)/shard_map/ppermute | solution.py:641
  163.4 16.8 %collective-permute-done.15.refs_8_ = bf16[2,128,512]{2,1,0:T(8,128)(2,1)S(1)} collective-permute-done((bf16[2,128,512]{2,1,0:T(8,128)(2,1)}, bf16[2,128,512]{2,1,0:T(8,128)(2,1)S(1)}, u32[]{:S(2)}, u32[]{:S(2)}) %collective-permute-start.15) | collective-permute-done | bytes 262176 | tf_op jit(solution)/shard_map/ppermute | solution.py:641
  180.9 13.8 %attend_last.1 = (bf16[8,384,512]{2,1,0:T(8,128)(2,1)}, bf16[8,128,512]{2,1,0:T(8,128)(2,1)}, f32[8,128,256]{2,1,0:T(8,128)}, bf16[6,128,256]{2,1,0:T(8,128)(2,1)}) custom-call(s32[34]{0:T(128)} %concatenate.7.refs_0_, bf16[2,128,1024]{2,1,0:T(8,128)(2,1)} %get-tuple-element.51.refs_1_, bf16[2,128,1024]{2,1,0:T(8,128)(2,1)} %copy-done.14, ...), custom_call_target="tpu_custom_call" | custom-call | flops 2684354560 | bytes 12582912 | tf_op jit(solution)/shard_map/attend_last/pallas_call | solution.py:414
  195.6 2.1 relay_out.1
  197.7 4.9 %all-to-all-start.2 = ((bf16[8,384,512]{2,1,0:T(8,128)(2,1)}), bf16[8,384,512]{2,1,0:T(8,128)(2,1)}, u32[]{:S(2)}, u32[]{:S(2)}) async-start(bf16[8,384,512]{2,1,0:T(8,128)(2,1)} %relay_out.1), calls=%async_computation.2 | async-start | bytes 6291456 | tf_op jit(solution)/shard_map/all_to_all | solution.py:638
  202.6 6.0 %collective-permute-start.23 = (bf16[6,128,256]{2,1,0:T(8,128)(2,1)S(1)}, bf16[6,128,256]{2,1,0:T(8,128)(2,1)S(1)}, u32[]{:S(2)}, u32[]{:S(2)}) collective-permute-start(bf16[6,128,256]{2,1,0:T(8,128)(2,1)S(1)} %copy-done.17), channel_id=1, source_target_pairs={{2,0},{3,1},{4,2},{5,3},{6,4},{7,5},{10,8},{11,9},{12,10},{13,11},... | collective-permute-start | bytes 1179656 | tf_op jit(solution)/shard_map/ppermute | solution.py:703
  208.6 8.3 %collective-permute-done.23.back_ref = bf16[6,128,256]{2,1,0:T(8,128)(2,1)S(1)} collective-permute-done((bf16[6,128,256]{2,1,0:T(8,128)(2,1)S(1)}, bf16[6,128,256]{2,1,0:T(8,128)(2,1)S(1)}, u32[]{:S(2)}, u32[]{:S(2)}) %collective-permute-start.23) | collective-permute-done | bytes 393248 | tf_op jit(solution)/shard_map/ppermute | solution.py:703
  217.7 2.9 %finish.1 = (bf16[128,768]{1,0:T(8,128)(2,1)}, bf16[128,768]{1,0:T(8,128)(2,1)}, bf16[128,768]{1,0:T(8,128)(2,1)}, bf16[128,768]{1,0:T(8,128)(2,1)}, bf16[128,76...) custom-call(s32[1]{0:T(128)} %bitcast.1.core_ref, ...), custom_call_target="tpu_custom_call" | custom-call | bytes 5242880 | tf_op jit(solution)/shard_map/finish/pallas_call | solution.py:460
  220.6 6.1 %collective-permute-start.24 = (bf16[128,768]{1,0:T(8,128)(2,1)}, bf16[128,768]{1,0:T(8,128)(2,1)S(1)}, u32[]{:S(2)}, u32[]{:S(2)}) collective-permute-start(bf16[128,768]{1,0:T(8,128)(2,1)} %get-tuple-element.85), channel_id=1, source_target_pairs={{0,0},{1,1},{2,8},{3,9},{4,16},{5,17},{6,24},{7,25},{8,2},{9,3},{1... | collective-permute-start | bytes 589832 | tf_op jit(solution)/shard_map/ppermute | solution.py:648
  227.7 3.5 %collective-permute-start.26 = (bf16[128,768]{1,0:T(8,128)(2,1)}, bf16[128,768]{1,0:T(8,128)(2,1)S(1)}, u32[]{:S(2)}, u32[]{:S(2)}) collective-permute-start(bf16[128,768]{1,0:T(8,128)(2,1)} %get-tuple-element.87), channel_id=1, source_target_pairs={{0,2},{1,3},{2,10},{3,11},{4,18},{5,19},{6,26},{7,27},{8,0},{9,1},... | collective-permute-start | bytes 589832 | tf_op jit(solution)/shard_map/ppermute | solution.py:648
  231.4 17.0 %collective-permute-done.24.refs_1_ = bf16[128,768]{1,0:T(8,128)(2,1)S(1)} collective-permute-done((bf16[128,768]{1,0:T(8,128)(2,1)}, bf16[128,768]{1,0:T(8,128)(2,1)S(1)}, u32[]{:S(2)}, u32[]{:S(2)}) %collective-permute-start.24) | collective-permute-done | bytes 196640 | tf_op jit(solution)/shard_map/ppermute | solution.py:648
  248.4 5.0 %collective-permute-done.25.refs_2_ = bf16[128,768]{1,0:T(8,128)(2,1)S(1)} collective-permute-done((bf16[128,768]{1,0:T(8,128)(2,1)}, bf16[128,768]{1,0:T(8,128)(2,1)S(1)}, u32[]{:S(2)}, u32[]{:S(2)}) %collective-permute-start.25) | collective-permute-done | bytes 196640 | tf_op jit(solution)/shard_map/ppermute | solution.py:648
  253.4 1.9 collective-permute-start.30
  255.4 1.5 collective-permute-done.26.refs_3_
  257.4 4.6 %collective-permute-done.27.refs_4_ = bf16[128,768]{1,0:T(8,128)(2,1)S(1)} collective-permute-done((bf16[128,768]{1,0:T(8,128)(2,1)}, bf16[128,768]{1,0:T(8,128)(2,1)S(1)}, u32[]{:S(2)}, u32[]{:S(2)}) %collective-permute-start.27) | collective-permute-done | bytes 196640 | tf_op jit(solution)/shard_map/ppermute | solution.py:648
  261.9 6.2 %collective-permute-done.29.refs_6_ = bf16[128,768]{1,0:T(8,128)(2,1)S(1)} collective-permute-done((bf16[128,768]{1,0:T(8,128)(2,1)}, bf16[128,768]{1,0:T(8,128)(2,1)S(1)}, u32[]{:S(2)}, u32[]{:S(2)}) %collective-permute-start.29) | collective-permute-done | bytes 196640 | tf_op jit(solution)/shard_map/ppermute | solution.py:648
  268.2 3.6 %collective-permute-done.30.refs_7_ = bf16[128,768]{1,0:T(8,128)(2,1)S(1)} collective-permute-done((bf16[128,768]{1,0:T(8,128)(2,1)}, bf16[128,768]{1,0:T(8,128)(2,1)S(1)}, u32[]{:S(2)}, u32[]{:S(2)}) %collective-permute-start.30) | collective-permute-done | bytes 196640 | tf_op jit(solution)/shard_map/ppermute | solution.py:648
  271.8 4.7 %collective-permute-done.31.refs_8_ = bf16[128,768]{1,0:T(8,128)(2,1)S(1)} collective-permute-done((bf16[128,768]{1,0:T(8,128)(2,1)}, bf16[128,768]{1,0:T(8,128)(2,1)S(1)}, u32[]{:S(2)}, u32[]{:S(2)}) %collective-permute-start.31) | collective-permute-done | bytes 196640 | tf_op jit(solution)/shard_map/ppermute | solution.py:648
  277.1 2.6 place_rows.1
  279.7 2.4 place_out.1._
  282.1 2.9 %place_last.1 = (bf16[256,8192]{1,0:T(8,128)(2,1)}, bf16[128,8192]{1,0:T(8,128)(2,1)}) custom-call(bf16[8,384,512]{2,1,0:T(8,128)(2,1)} %all-to-all-done.2.in_ref, bf16[256,8192]{1,0:T(8,128)(2,1)} %place_out.1._, bf16[128,8192]{1,0:T(8,128)(2,1)} %get-tuple-element.93.__), custom_call_target="tpu_custom_call", output_to_operand_aliasing={{0}: (1, {}), {1}: (2, {})} | custom-call | bytes 6291456 | tf_op jit(solution)/shard_map/place_last/pallas_call | solution.py:565
  (111 shorter events, 14.6 us)
Async XLA Ops:
  0.6 39.6 %copy-start = (s32[4,4,4]{2,1,0:T(4,128)S(1)}, s32[4,4,4]{2,1,0:T(4,128)}, u32[]{:S(2)}) copy-start(s32[4,4,4]{2,1,0:T(4,128)} %param.11) | copy-start | bytes 772
  3.1 24.4 %all-to-all-start = ((bf16[8,128,768]{2,1,0:T(8,128)(2,1)}), bf16[8,128,768]{2,1,0:T(8,128)(2,1)S(1)}, u32[]{:S(2)}, u32[]{:S(2)}) async-start(bf16[8,128,768]{2,1,0:T(8,128)(2,1)} %shard_map.93), calls=%async_computation | async-start | bytes 3145728 | tf_op jit(solution)/shard_map/all_to_all | solution.py:638
  9.9 27.2 %collective-permute-start.3 = (bf16[256,512]{1,0:T(8,128)(2,1)}, bf16[256,512]{1,0:T(8,128)(2,1)S(1)}, u32[]{:S(2)}, u32[]{:S(2)}) collective-permute-start(bf16[256,512]{1,0:T(8,128)(2,1)} %get-tuple-element.56), channel_id=1, source_target_pairs={{0,1},{1,0},{2,3},{3,2},{4,5},{5,4},{6,7},{7,6},{8,9},{9,8},{10,11... | collective-permute-start | bytes 786440 | tf_op jit(solution)/shard_map/ppermute | solution.py:669
  11.3 27.1 %collective-permute-start.4 = (bf16[256,512]{1,0:T(8,128)(2,1)}, bf16[256,512]{1,0:T(8,128)(2,1)}, u32[]{:S(2)}, u32[]{:S(2)}) collective-permute-start(bf16[256,512]{1,0:T(8,128)(2,1)} %get-tuple-element.57), channel_id=1, source_target_pairs={{0,8},{1,9},{2,10},{3,11},{4,12},{5,13},{6,14},{7,15},{8,0},{9,1},... | collective-permute-start | bytes 786440 | tf_op jit(solution)/shard_map/ppermute | solution.py:669
  12.0 27.1 %collective-permute-start.5 = (bf16[256,512]{1,0:T(8,128)(2,1)}, bf16[256,512]{1,0:T(8,128)(2,1)}, u32[]{:S(2)}, u32[]{:S(2)}) collective-permute-start(bf16[256,512]{1,0:T(8,128)(2,1)} %get-tuple-element.58), channel_id=1, source_target_pairs={{0,9},{1,8},{2,11},{3,10},{4,13},{5,12},{6,15},{7,14},{8,1},{9,0},... | collective-permute-start | bytes 786440 | tf_op jit(solution)/shard_map/ppermute | solution.py:669
  14.1 45.4 %copy-start.33 = (s32[32]{0:T(128)S(1)}, s32[32]{0:T(128)}, u32[]{:S(2)}) copy-start(s32[32]{0:T(128)} %param.10) | copy-start | bytes 388
  27.5 71.8 %all-to-all-start.1 = ((bf16[8,128,512]{2,1,0:T(8,128)(2,1)}), bf16[8,128,512]{2,1,0:T(8,128)(2,1)}, u32[]{:S(2)}, u32[]{:S(2)}) async-start(bf16[8,128,512]{2,1,0:T(8,128)(2,1)} %shard_map.94), calls=%async_computation.1 | async-start | bytes 2097152 | tf_op jit(solution)/shard_map/all_to_all | solution.py:638
  32.0 24.8 %collective-permute-start.6 = (bf16[256,512]{1,0:T(8,128)(2,1)}, bf16[256,512]{1,0:T(8,128)(2,1)}, u32[]{:S(2)}, u32[]{:S(2)}) collective-permute-start(bf16[256,512]{1,0:T(8,128)(2,1)} %get-tuple-element.59), channel_id=1, source_target_pairs={{0,16},{1,17},{2,18},{3,19},{4,20},{5,21},{6,22},{7,23},{8,24},{9,... | collective-permute-start | bytes 786440 | tf_op jit(solution)/shard_map/ppermute | solution.py:669
  33.4 24.4 %collective-permute-start.7 = (bf16[256,512]{1,0:T(8,128)(2,1)}, bf16[256,512]{1,0:T(8,128)(2,1)}, u32[]{:S(2)}, u32[]{:S(2)}) collective-permute-start(bf16[256,512]{1,0:T(8,128)(2,1)} %get-tuple-element.60), channel_id=1, source_target_pairs={{0,17},{1,16},{2,19},{3,18},{4,21},{5,20},{6,23},{7,22},{8,25},{9,... | collective-permute-start | bytes 786440 | tf_op jit(solution)/shard_map/ppermute | solution.py:669
  37.1 34.3 %collective-permute-start = (bf16[2,128,1024]{2,1,0:T(8,128)(2,1)}, bf16[2,128,1024]{2,1,0:T(8,128)(2,1)S(1)}, u32[]{:S(2)}, u32[]{:S(2)}) collective-permute-start(bf16[2,128,1024]{2,1,0:T(8,128)(2,1)} %get-tuple-element.52), channel_id=1, source_target_pairs={{0,2},{1,3},{2,0},{3,1},{4,6},{5,7},{6,4},{7,5},{8,10},{9,11},{10,... | collective-permute-start | bytes 1572872 | tf_op jit(solution)/shard_map/ppermute | solution.py:641
  38.4 32.9 %collective-permute-start.1 = (bf16[2,128,1024]{2,1,0:T(8,128)(2,1)}, bf16[2,128,1024]{2,1,0:T(8,128)(2,1)S(1)}, u32[]{:S(2)}, u32[]{:S(2)}) collective-permute-start(bf16[2,128,1024]{2,1,0:T(8,128)(2,1)} %get-tuple-element.53), channel_id=1, source_target_pairs={{0,4},{1,5},{2,6},{3,7},{4,0},{5,1},{6,2},{7,3},{8,12},{9,13},{10,... | collective-permute-start | bytes 1572872 | tf_op jit(solution)/shard_map/ppermute | solution.py:641
  39.1 46.2 %collective-permute-start.2 = (bf16[2,128,1024]{2,1,0:T(8,128)(2,1)}, bf16[2,128,1024]{2,1,0:T(8,128)(2,1)S(1)}, u32[]{:S(2)}, u32[]{:S(2)}) collective-permute-start(bf16[2,128,1024]{2,1,0:T(8,128)(2,1)} %get-tuple-element.54), channel_id=1, source_target_pairs={{0,6},{1,7},{2,4},{3,5},{4,2},{5,3},{6,0},{7,1},{8,14},{9,15},{10,... | collective-permute-start | bytes 1572872 | tf_op jit(solution)/shard_map/ppermute | solution.py:641
  56.9 14.5 %collective-permute-start.8 = (bf16[256,512]{1,0:T(8,128)(2,1)}, bf16[256,512]{1,0:T(8,128)(2,1)S(1)}, u32[]{:S(2)}, u32[]{:S(2)}) collective-permute-start(bf16[256,512]{1,0:T(8,128)(2,1)} %get-tuple-element.61), channel_id=1, source_target_pairs={{0,24},{1,25},{2,26},{3,27},{4,28},{5,29},{6,30},{7,31},{8,16},{9,... | collective-permute-start | bytes 786440 | tf_op jit(solution)/shard_map/ppermute | solution.py:669
  57.8 13.5 %collective-permute-start.9 = (bf16[256,512]{1,0:T(8,128)(2,1)}, bf16[256,512]{1,0:T(8,128)(2,1)S(1)}, u32[]{:S(2)}, u32[]{:S(2)}) collective-permute-start(bf16[256,512]{1,0:T(8,128)(2,1)} %get-tuple-element.62), channel_id=1, source_target_pairs={{0,25},{1,24},{2,27},{3,26},{4,29},{5,28},{6,31},{7,30},{8,17},{9,... | collective-permute-start | bytes 786440 | tf_op jit(solution)/shard_map/ppermute | solution.py:669
  99.4 98.3 %all-to-all-start.3 = ((bf16[8,256,512]{2,1,0:T(8,128)(2,1)}), bf16[8,256,512]{2,1,0:T(8,128)(2,1)}, u32[]{:S(2)}, u32[]{:S(2)}) async-start(bf16[8,256,512]{2,1,0:T(8,128)(2,1)} %get-tuple-element.81), calls=%async_computation.3 | async-start | bytes 4194304 | tf_op jit(solution)/shard_map/all_to_all | solution.py:638
  105.4 51.6 %copy-start.20 = (bf16[2,128,512]{2,1,0:T(8,128)(2,1)S(1)}, bf16[2,128,512]{2,1,0:T(8,128)(2,1)}, u32[]{:S(2)}) copy-start(bf16[2,128,512]{2,1,0:T(8,128)(2,1)} %get-tuple-element.64) | copy-start | bytes 786436
  105.4 51.7 %copy-start.19 = (bf16[2,128,512]{2,1,0:T(8,128)(2,1)S(1)}, bf16[2,128,512]{2,1,0:T(8,128)(2,1)}, u32[]{:S(2)}) copy-start(bf16[2,128,512]{2,1,0:T(8,128)(2,1)} %get-tuple-element.65) | copy-start | bytes 786436
  105.4 54.8 %copy-start.18 = (bf16[2,128,512]{2,1,0:T(8,128)(2,1)S(1)}, bf16[2,128,512]{2,1,0:T(8,128)(2,1)}, u32[]{:S(2)}) copy-start(bf16[2,128,512]{2,1,0:T(8,128)(2,1)} %get-tuple-element.66) | copy-start | bytes 786436
  107.9 27.8 %collective-permute-start.16 = (bf16[256,512]{1,0:T(8,128)(2,1)}, bf16[256,512]{1,0:T(8,128)(2,1)S(1)}, u32[]{:S(2)}, u32[]{:S(2)}) collective-permute-start(bf16[256,512]{1,0:T(8,128)(2,1)} %get-tuple-element.72), channel_id=1, source_target_pairs={{0,1},{1,0},{2,3},{3,2},{4,5},{5,4},{6,7},{7,6},{8,9},{9,8},{10,11... | collective-permute-start | bytes 786440 | tf_op jit(solution)/shard_map/ppermute | solution.py:669
  109.3 29.0 %collective-permute-start.17 = (bf16[256,512]{1,0:T(8,128)(2,1)}, bf16[256,512]{1,0:T(8,128)(2,1)S(1)}, u32[]{:S(2)}, u32[]{:S(2)}) collective-permute-start(bf16[256,512]{1,0:T(8,128)(2,1)} %get-tuple-element.73), channel_id=1, source_target_pairs={{0,8},{1,9},{2,10},{3,11},{4,12},{5,13},{6,14},{7,15},{8,0},{9,1},... | collective-permute-start | bytes 786440 | tf_op jit(solution)/shard_map/ppermute | solution.py:669
  110.0 32.5 %collective-permute-start.18 = (bf16[256,512]{1,0:T(8,128)(2,1)}, bf16[256,512]{1,0:T(8,128)(2,1)S(1)}, u32[]{:S(2)}, u32[]{:S(2)}) collective-permute-start(bf16[256,512]{1,0:T(8,128)(2,1)} %get-tuple-element.74), channel_id=1, source_target_pairs={{0,9},{1,8},{2,11},{3,10},{4,13},{5,12},{6,15},{7,14},{8,1},{9,0},... | collective-permute-start | bytes 786440 | tf_op jit(solution)/shard_map/ppermute | solution.py:669
  110.0 32.5 %collective-permute-start.19 = (bf16[256,512]{1,0:T(8,128)(2,1)}, bf16[256,512]{1,0:T(8,128)(2,1)S(1)}, u32[]{:S(2)}, u32[]{:S(2)}) collective-permute-start(bf16[256,512]{1,0:T(8,128)(2,1)} %get-tuple-element.75), channel_id=1, source_target_pairs={{0,16},{1,17},{2,18},{3,19},{4,20},{5,21},{6,22},{7,23},{8,24},{9,... | collective-permute-start | bytes 786440 | tf_op jit(solution)/shard_map/ppermute | solution.py:669
  111.4 36.7 %collective-permute-start.20 = (bf16[256,512]{1,0:T(8,128)(2,1)}, bf16[256,512]{1,0:T(8,128)(2,1)}, u32[]{:S(2)}, u32[]{:S(2)}) collective-permute-start(bf16[256,512]{1,0:T(8,128)(2,1)} %get-tuple-element.76), channel_id=1, source_target_pairs={{0,17},{1,16},{2,19},{3,18},{4,21},{5,20},{6,23},{7,22},{8,25},{9,... | collective-permute-start | bytes 786440 | tf_op jit(solution)/shard_map/ppermute | solution.py:669
  135.7 45.2 %copy-start.22 = (bf16[256,512]{1,0:T(8,128)(2,1)}, bf16[256,512]{1,0:T(8,128)(2,1)S(1)}, u32[]{:S(2)}) copy-start(bf16[256,512]{1,0:T(8,128)(2,1)S(1)} %collective-permute-done.16.refs_10_) | copy-start | bytes 786436
  135.7 21.2 %collective-permute-start.21 = (bf16[256,512]{1,0:T(8,128)(2,1)}, bf16[256,512]{1,0:T(8,128)(2,1)S(1)}, u32[]{:S(2)}, u32[]{:S(2)}) collective-permute-start(bf16[256,512]{1,0:T(8,128)(2,1)} %get-tuple-element.77), channel_id=1, source_target_pairs={{0,24},{1,25},{2,26},{3,27},{4,28},{5,29},{6,30},{7,31},{8,16},{9,... | collective-permute-start | bytes 786440 | tf_op jit(solution)/shard_map/ppermute | solution.py:669
  138.3 18.6 %copy-start.23 = (bf16[256,512]{1,0:T(8,128)(2,1)}, bf16[256,512]{1,0:T(8,128)(2,1)S(1)}, u32[]{:S(2)}) copy-start(bf16[256,512]{1,0:T(8,128)(2,1)S(1)} %collective-permute-done.17.refs_11_) | copy-start | bytes 786436
  138.3 18.6 %collective-permute-start.22 = (bf16[256,512]{1,0:T(8,128)(2,1)}, bf16[256,512]{1,0:T(8,128)(2,1)S(1)}, u32[]{:S(2)}, u32[]{:S(2)}) collective-permute-start(bf16[256,512]{1,0:T(8,128)(2,1)} %get-tuple-element.78), channel_id=1, source_target_pairs={{0,25},{1,24},{2,27},{3,26},{4,29},{5,28},{6,31},{7,30},{8,17},{9,... | collective-permute-start | bytes 786440 | tf_op jit(solution)/shard_map/ppermute | solution.py:669
  142.5 17.7 %collective-permute-start.13 = (bf16[2,128,512]{2,1,0:T(8,128)(2,1)}, bf16[2,128,512]{2,1,0:T(8,128)(2,1)S(1)}, u32[]{:S(2)}, u32[]{:S(2)}) collective-permute-start(bf16[2,128,512]{2,1,0:T(8,128)(2,1)} %get-tuple-element.68), channel_id=1, source_target_pairs={{0,2},{1,3},{2,0},{3,1},{4,6},{5,7},{6,4},{7,5},{8,10},{9,11},{10,... | collective-permute-start | bytes 786440 | tf_op jit(solution)/shard_map/ppermute | solution.py:641
  142.5 17.7 %copy-start.25 = (bf16[256,512]{1,0:T(8,128)(2,1)}, bf16[256,512]{1,0:T(8,128)(2,1)S(1)}, u32[]{:S(2)}) copy-start(bf16[256,512]{1,0:T(8,128)(2,1)S(1)} %collective-permute-done.19.refs_13_) | copy-start | bytes 786436
  142.5 20.9 %collective-permute-start.14 = (bf16[2,128,512]{2,1,0:T(8,128)(2,1)}, bf16[2,128,512]{2,1,0:T(8,128)(2,1)S(1)}, u32[]{:S(2)}, u32[]{:S(2)}) collective-permute-start(bf16[2,128,512]{2,1,0:T(8,128)(2,1)} %get-tuple-element.69), channel_id=1, source_target_pairs={{0,4},{1,5},{2,6},{3,7},{4,0},{5,1},{6,2},{7,3},{8,12},{9,13},{10,... | collective-permute-start | bytes 786440 | tf_op jit(solution)/shard_map/ppermute | solution.py:641
  148.0 32.2 %collective-permute-start.15 = (bf16[2,128,512]{2,1,0:T(8,128)(2,1)}, bf16[2,128,512]{2,1,0:T(8,128)(2,1)S(1)}, u32[]{:S(2)}, u32[]{:S(2)}) collective-permute-start(bf16[2,128,512]{2,1,0:T(8,128)(2,1)} %get-tuple-element.70), channel_id=1, source_target_pairs={{0,6},{1,7},{2,4},{3,5},{4,2},{5,3},{6,0},{7,1},{8,14},{9,15},{10,... | collective-permute-start | bytes 786440 | tf_op jit(solution)/shard_map/ppermute | solution.py:641
  156.9 37.8 %collective-permute-start.10 = (bf16[2,128,512]{2,1,0:T(8,128)(2,1)S(1)}, bf16[2,128,512]{2,1,0:T(8,128)(2,1)S(1)}, u32[]{:S(2)}, u32[]{:S(2)}) collective-permute-start(bf16[2,128,512]{2,1,0:T(8,128)(2,1)S(1)} %copy-done.20), channel_id=1, source_target_pairs={{0,2},{1,3},{2,0},{3,1},{4,6},{5,7},{6,4},{7,5},{8,10},{9,11},{10,... | collective-permute-start | bytes 786440 | tf_op jit(solution)/shard_map/ppermute | solution.py:641
  157.0 37.7 %collective-permute-start.11 = (bf16[2,128,512]{2,1,0:T(8,128)(2,1)S(1)}, bf16[2,128,512]{2,1,0:T(8,128)(2,1)S(1)}, u32[]{:S(2)}, u32[]{:S(2)}) collective-permute-start(bf16[2,128,512]{2,1,0:T(8,128)(2,1)S(1)} %copy-done.19), channel_id=1, source_target_pairs={{0,4},{1,5},{2,6},{3,7},{4,0},{5,1},{6,2},{7,3},{8,12},{9,13},{10,... | collective-permute-start | bytes 786440 | tf_op jit(solution)/shard_map/ppermute | solution.py:641
  160.2 20.1 %copy-start.28 = (bf16[2,128,512]{2,1,0:T(8,128)(2,1)}, bf16[2,128,512]{2,1,0:T(8,128)(2,1)S(1)}, u32[]{:S(2)}) copy-start(bf16[2,128,512]{2,1,0:T(8,128)(2,1)S(1)} %collective-permute-done.13.refs_6_) | copy-start | bytes 786436
  160.2 34.6 %collective-permute-start.12 = (bf16[2,128,512]{2,1,0:T(8,128)(2,1)S(1)}, bf16[2,128,512]{2,1,0:T(8,128)(2,1)S(1)}, u32[]{:S(2)}, u32[]{:S(2)}) collective-permute-start(bf16[2,128,512]{2,1,0:T(8,128)(2,1)S(1)} %copy-done.18), channel_id=1, source_target_pairs={{0,6},{1,7},{2,4},{3,5},{4,2},{5,3},{6,0},{7,1},{8,14},{9,15},{10,... | collective-permute-start | bytes 786440 | tf_op jit(solution)/shard_map/ppermute | solution.py:641
  197.7 84.4 %all-to-all-start.2 = ((bf16[8,384,512]{2,1,0:T(8,128)(2,1)}), bf16[8,384,512]{2,1,0:T(8,128)(2,1)}, u32[]{:S(2)}, u32[]{:S(2)}) async-start(bf16[8,384,512]{2,1,0:T(8,128)(2,1)} %relay_out.1), calls=%async_computation.2 | async-start | bytes 6291456 | tf_op jit(solution)/shard_map/all_to_all | solution.py:638
  202.6 14.4 %collective-permute-start.23 = (bf16[6,128,256]{2,1,0:T(8,128)(2,1)S(1)}, bf16[6,128,256]{2,1,0:T(8,128)(2,1)S(1)}, u32[]{:S(2)}, u32[]{:S(2)}) collective-permute-start(bf16[6,128,256]{2,1,0:T(8,128)(2,1)S(1)} %copy-done.17), channel_id=1, source_target_pairs={{2,0},{3,1},{4,2},{5,3},{6,4},{7,5},{10,8},{11,9},{12,10},{13,11},... | collective-permute-start | bytes 1179656 | tf_op jit(solution)/shard_map/ppermute | solution.py:703
  220.6 27.8 %collective-permute-start.24 = (bf16[128,768]{1,0:T(8,128)(2,1)}, bf16[128,768]{1,0:T(8,128)(2,1)S(1)}, u32[]{:S(2)}, u32[]{:S(2)}) collective-permute-start(bf16[128,768]{1,0:T(8,128)(2,1)} %get-tuple-element.85), channel_id=1, source_target_pairs={{0,0},{1,1},{2,8},{3,9},{4,16},{5,17},{6,24},{7,25},{8,2},{9,3},{1... | collective-permute-start | bytes 589832 | tf_op jit(solution)/shard_map/ppermute | solution.py:648
  226.7 26.8 %collective-permute-start.25 = (bf16[128,768]{1,0:T(8,128)(2,1)}, bf16[128,768]{1,0:T(8,128)(2,1)S(1)}, u32[]{:S(2)}, u32[]{:S(2)}) collective-permute-start(bf16[128,768]{1,0:T(8,128)(2,1)} %get-tuple-element.86), channel_id=1, source_target_pairs={{0,1},{1,0},{2,9},{3,8},{4,17},{5,16},{6,25},{7,24},{8,3},{9,2},{1... | collective-permute-start | bytes 589832 | tf_op jit(solution)/shard_map/ppermute | solution.py:648
  227.7 29.2 %collective-permute-start.26 = (bf16[128,768]{1,0:T(8,128)(2,1)}, bf16[128,768]{1,0:T(8,128)(2,1)S(1)}, u32[]{:S(2)}, u32[]{:S(2)}) collective-permute-start(bf16[128,768]{1,0:T(8,128)(2,1)} %get-tuple-element.87), channel_id=1, source_target_pairs={{0,2},{1,3},{2,10},{3,11},{4,18},{5,19},{6,26},{7,27},{8,0},{9,1},... | collective-permute-start | bytes 589832 | tf_op jit(solution)/shard_map/ppermute | solution.py:648
  231.2 30.7 %collective-permute-start.27 = (bf16[128,768]{1,0:T(8,128)(2,1)}, bf16[128,768]{1,0:T(8,128)(2,1)S(1)}, u32[]{:S(2)}, u32[]{:S(2)}) collective-permute-start(bf16[128,768]{1,0:T(8,128)(2,1)} %get-tuple-element.88), channel_id=1, source_target_pairs={{0,3},{1,2},{2,11},{3,10},{4,19},{5,18},{6,27},{7,26},{8,1},{9,0},... | collective-permute-start | bytes 589832 | tf_op jit(solution)/shard_map/ppermute | solution.py:648
  231.4 30.5 %collective-permute-start.28 = (bf16[128,768]{1,0:T(8,128)(2,1)}, bf16[128,768]{1,0:T(8,128)(2,1)S(1)}, u32[]{:S(2)}, u32[]{:S(2)}) collective-permute-start(bf16[128,768]{1,0:T(8,128)(2,1)} %get-tuple-element.89), channel_id=1, source_target_pairs={{0,4},{1,5},{2,12},{3,13},{4,20},{5,21},{6,28},{7,29},{8,6},{9,7},... | collective-permute-start | bytes 589832 | tf_op jit(solution)/shard_map/ppermute | solution.py:648
  248.4 28.0 %copy-start.6 = (bf16[128,768]{1,0:T(8,128)(2,1)}, bf16[128,768]{1,0:T(8,128)(2,1)S(1)}, u32[]{:S(2)}) copy-start(bf16[128,768]{1,0:T(8,128)(2,1)S(1)} %collective-permute-done.24.refs_1_) | copy-start | bytes 589828
  248.4 19.7 %collective-permute-start.29 = (bf16[128,768]{1,0:T(8,128)(2,1)}, bf16[128,768]{1,0:T(8,128)(2,1)S(1)}, u32[]{:S(2)}, u32[]{:S(2)}) collective-permute-start(bf16[128,768]{1,0:T(8,128)(2,1)} %get-tuple-element.90), channel_id=1, source_target_pairs={{0,5},{1,4},{2,13},{3,12},{4,21},{5,20},{6,29},{7,28},{8,7},{9,6},... | collective-permute-start | bytes 589832 | tf_op jit(solution)/shard_map/ppermute | solution.py:648
  253.4 23.0 %copy-start.7 = (bf16[128,768]{1,0:T(8,128)(2,1)}, bf16[128,768]{1,0:T(8,128)(2,1)S(1)}, u32[]{:S(2)}) copy-start(bf16[128,768]{1,0:T(8,128)(2,1)S(1)} %collective-permute-done.25.refs_2_) | copy-start | bytes 589828
  253.4 18.3 %collective-permute-start.30 = (bf16[128,768]{1,0:T(8,128)(2,1)}, bf16[128,768]{1,0:T(8,128)(2,1)S(1)}, u32[]{:S(2)}, u32[]{:S(2)}) collective-permute-start(bf16[128,768]{1,0:T(8,128)(2,1)} %get-tuple-element.91), channel_id=1, source_target_pairs={{0,6},{1,7},{2,14},{3,15},{4,22},{5,23},{6,30},{7,31},{8,4},{9,5},... | collective-permute-start | bytes 589832 | tf_op jit(solution)/shard_map/ppermute | solution.py:648
  256.8 19.6 %copy-start.8 = (bf16[128,768]{1,0:T(8,128)(2,1)}, bf16[128,768]{1,0:T(8,128)(2,1)S(1)}, u32[]{:S(2)}) copy-start(bf16[128,768]{1,0:T(8,128)(2,1)S(1)} %collective-permute-done.26.refs_3_) | copy-start | bytes 589828
  256.8 19.6 %collective-permute-start.31 = (bf16[128,768]{1,0:T(8,128)(2,1)}, bf16[128,768]{1,0:T(8,128)(2,1)S(1)}, u32[]{:S(2)}, u32[]{:S(2)}) collective-permute-start(bf16[128,768]{1,0:T(8,128)(2,1)} %get-tuple-element.92), channel_id=1, source_target_pairs={{0,7},{1,6},{2,15},{3,14},{4,23},{5,22},{6,31},{7,30},{8,5},{9,4},... | collective-permute-start | bytes 589832 | tf_op jit(solution)/shard_map/ppermute | solution.py:648
  (22 other events, 157.7 us)

commit v2 on v1

--- a/solution.py
+++ b/solution.py
@@ -475,15 +475,16 @@
     )(core_index, rows, main, back)
 
 
-def place_rows(block_index, last_rows, groups):
+def place_last(block_index, last_rows, parts, out, groups):
     repeats = groups // KVH
-    width = QH // groups * DH
-    half = width // CHUNKS
+    _, total, half = parts.shape
+    width = 2 * half
+    rows = total - BLOCK
 
     def kernel(*refs):
         at_ref, *refs = refs
         lasts, refs = refs[:groups], refs[groups:]
-        gq_ref, gk_ref, gv_ref, rows, held, sums, sem_in, sem_out = refs
+        in_ref, _, out_ref, gq_ref, gk_ref, gv_ref, buf, ends, held, sums, sem_in, sem_out = refs
         at = at_ref[0]
         loads, stores = [], []
 
@@ -498,88 +499,56 @@
             stores.append(copy)
 
         for k in range(groups):
-            load(lasts[k].at[:, :half], rows.at[k])
             load(lasts[k].at[:, half:], held.at[at ^ k])
         for k in range(groups):
-            col = pl.multiple_of((at ^ k) * width + half, half)
-            loads[2 * k].wait()
-            store(rows.at[k], gq_ref.at[:, pl.ds(col, half)])
+            load(lasts[k].at[:, :half], ends.at[k])
+        for r in range(groups):
+            load(in_ref.at[r], buf.at[r])
         for k in range(groups):
-            loads[2 * k + 1].wait()
+            loads[k].wait()
         for head in range(KVH):
-            total = held[head * repeats].astype(F32)
+            term = held[head * repeats].astype(F32)
             for extra in range(1, repeats):
-                total += held[head * repeats + extra].astype(F32)
-            sums[0, :, head * DH : (head + 1) * DH] = total[:, :DH].astype(BF16)
-            sums[1, :, head * DH : (head + 1) * DH] = total[:, DH:].astype(BF16)
+                term += held[head * repeats + extra].astype(F32)
+            sums[0, :, head * DH : (head + 1) * DH] = term[:, :DH].astype(BF16)
+            sums[1, :, head * DH : (head + 1) * DH] = term[:, DH:].astype(BF16)
         store(sums.at[0], gk_ref)
         store(sums.at[1], gv_ref)
+        for k in range(groups):
+            col = pl.multiple_of((at ^ k) * width + half, half)
+            loads[groups + k].wait()
+            store(ends.at[k], gq_ref.at[:, pl.ds(col, half)])
+        for r in range(groups):
+            first, second = 2 * r * half, (2 * r + 1) * half
+            loads[2 * groups + r].wait()
+            store(buf.at[r, :rows, :], out_ref.at[:, second : second + half])
+            store(buf.at[r, rows:, :], gq_ref.at[:, first : first + half])
         for copy in stores:
             copy.wait()
 
     return pl.pallas_call(
         kernel,
-        in_specs=[pl.BlockSpec(memory_space=pltpu.SMEM)] + [ANY] * groups,
-        out_specs=[ANY] * 3,
+        in_specs=[pl.BlockSpec(memory_space=pltpu.SMEM)] + [ANY] * (groups + 2),
+        out_specs=[ANY] * 4,
         out_shape=[
+            jax.ShapeDtypeStruct(out.shape, BF16),
             jax.ShapeDtypeStruct((BLOCK, QH * DH), BF16),
             jax.ShapeDtypeStruct((BLOCK, KVH * DH), BF16),
             jax.ShapeDtypeStruct((BLOCK, KVH * DH), BF16),
         ],
         scratch_shapes=[
+            pltpu.VMEM((groups, total, half), BF16),
             pltpu.VMEM((groups, BLOCK, half), BF16),
             pltpu.VMEM((groups, BLOCK, 2 * DH), BF16),
             pltpu.VMEM((2, BLOCK, KVH * DH), BF16),
-            pltpu.SemaphoreType.DMA((2 * groups,)),
-            pltpu.SemaphoreType.DMA((groups + 2,)),
+            pltpu.SemaphoreType.DMA((3 * groups,)),
+            pltpu.SemaphoreType.DMA((3 * groups + 2,)),
         ],
-        cost_estimate=pl.CostEstimate(flops=0, bytes_accessed=4 << 20, transcendentals=0),
-        compiler_params=pltpu.CompilerParams(vmem_limit_bytes=62 << 20),
-        name="place_rows",
-    )(block_index, *last_rows)
-
-
-def place_last(parts, out, grad_query):
-    groups, total, half = parts.shape
-    rows = total - BLOCK
-
-    def kernel(in_ref, _, __, out_ref, gq_ref, buf, sem_in, sem_out):
-        loads = [pltpu.make_async_copy(in_ref.at[r], buf.at[r], sem_in.at[r]) for r in range(groups)]
-        stores = []
-        for copy in loads:
-            copy.start()
-        for r in range(groups):
-            first, second = 2 * r * half, (2 * r + 1) * half
-            loads[r].wait()
-            pairs = [
-                (buf.at[r, :rows, :], out_ref.at[:, second : second + half]),
-                (buf.at[r, rows:, :], gq_ref.at[:, first : first + half]),
-            ]
-            for n, (src, dst) in enumerate(pairs):
-                copy = pltpu.make_async_copy(src, dst, sem_out.at[2 * r + n])
-                copy.start()
-                stores.append(copy)
-        for copy in stores:
-            copy.wait()
-
-    return pl.pallas_call(
-        kernel,
-        in_specs=[ANY] * 3,
-        out_specs=[ANY] * 2,
-        out_shape=[
-            jax.ShapeDtypeStruct(out.shape, BF16),
-            jax.ShapeDtypeStruct(grad_query.shape, BF16),
-        ],
-        scratch_shapes=[
-            pltpu.VMEM((groups, total, half), BF16),
-            pltpu.SemaphoreType.DMA((groups,)),
-            pltpu.SemaphoreType.DMA((2 * groups,)),
-        ],
-        input_output_aliases={1: 0, 2: 1},
-        cost_estimate=pl.CostEstimate(flops=0, bytes_accessed=6 << 20, transcendentals=0),
+        input_output_aliases={groups + 2: 0},
+        cost_estimate=pl.CostEstimate(flops=0, bytes_accessed=10 << 20, transcendentals=0),
         compiler_params=pltpu.CompilerParams(vmem_limit_bytes=62 << 20),
         name="place_last",
-    )(parts, out, grad_query)
+    )(block_index, *last_rows, parts, out)
 
 
 def place_out(parts):
@@ -710,8 +679,9 @@
 
     attn_out = place_out(back_first)
     block_index = (plane * per_plane + part).astype(jnp.int32).reshape(1)
-    grad_query, grad_key, grad_value = place_rows(block_index, home_second, groups)
-    attn_out, grad_query = place_last(back_second, attn_out, grad_query)
+    attn_out, grad_query, grad_key, grad_value = place_last(
+        block_index, home_second, back_second, attn_out, groups
+    )
     return (attn_out, grad_query, grad_key, grad_value)
 
 

time: 286 us -> 282 us (0.986)
  waiting for transfers between devices: 161 us -> 158 us
  transfers between devices with their start and end apart: 36 -> 36, of which waited for: 19 -> 19; matrix products, arithmetic and copies ran while one was open for 0% -> 0% of each run, Pallas kernels for 17% -> 16%
where the time goes in v2:
time: 282 us
  waiting for transfers between devices  158 us (56%)
  starting transfers between devices  64.9 us (23%)
  Pallas kernels  52.6 us (19%)
  local copies, waits for them, and re-layouts  4.65 us (2%)
    ppermute x14, waiting for transfers between devices, across(): return lax.ppermute(x, axes, pairs)  62.4 us
    ppermute x8, waiting for transfers between devices, home(): return lax.ppermute(x, axes, pairs)  40.1 us
    ppermute x9, waiting for transfers between devices, along(): lax.ppermute(x, axes, [(device(a, b, c), device(a, b ^ k, c)) for a, b, c...  33.9 us
    pallas_call x2, Pallas kernels, attend(): pl.pallas_call(kernel, in_specs=[pl.BlockSpec(memory_space=pltpu.SMEM)] +...  27 us
    all_to_all x4, starting transfers between devices, swap(): lax.all_to_all(x, plane_axes, split_axis=0, concat_axis=0, tiled=True)  19.8 us
    ppermute x14, starting transfers between devices, across(): return lax.ppermute(x, axes, pairs)  14.6 us
    all_to_all x4, waiting for transfers between devices, swap(): lax.all_to_all(x, plane_axes, split_axis=0, concat_axis=0, tiled=True)  13.4 us
    ppermute x8, starting transfers between devices, home(): return lax.ppermute(x, axes, pairs)  13.3 us
  transfers between devices with their start and end apart: 36, of which 19 were waited for; matrix products, arithmetic and copies ran while one was open for 0% of the time, Pallas kernels for 16%

profile of v2, /device:TPU:17, one launch (start us, length us, event | category | flops | bytes accessed | tf_op | source)
XLA Modules:
  0.0 281.6 jit_solution(10877612399500965926)
XLA Ops:
  0.6 2.4 shard_map.93
  3.1 4.4 %all-to-all-start = ((bf16[8,128,768]{2,1,0:T(8,128)(2,1)}), bf16[8,128,768]{2,1,0:T(8,128)(2,1)S(1)}, u32[]{:S(2)}, u32[]{:S(2)}) async-start(bf16[8,128,768]{2,1,0:T(8,128)(2,1)} %shard_map.93), calls=%async_computation | async-start | bytes 3145728 | tf_op jit(solution)/shard_map/all_to_all | solution.py:607
  7.5 2.4 pack_grad.3
  9.9 1.4 collective-permute-start.13
  12.0 2.1 shard_map.94
  14.1 13.4 %all-to-all-done = bf16[8,128,768]{2,1,0:T(8,128)(2,1)S(1)} async-done(((bf16[8,128,768]{2,1,0:T(8,128)(2,1)}), bf16[8,128,768]{2,1,0:T(8,128)(2,1)S(1)}, u32[]{:S(2)}, u32[]{:S(2)}) %all-to-all-start) | async-done | bytes 1572896 | tf_op jit(solution)/shard_map/all_to_all | solution.py:607
  27.5 4.5 %all-to-all-start.1 = ((bf16[8,128,512]{2,1,0:T(8,128)(2,1)}), bf16[8,128,512]{2,1,0:T(8,128)(2,1)}, u32[]{:S(2)}, u32[]{:S(2)}) async-start(bf16[8,128,512]{2,1,0:T(8,128)(2,1)} %shard_map.94), calls=%async_computation.1 | async-start | bytes 2097152 | tf_op jit(solution)/shard_map/all_to_all | solution.py:607
  32.0 1.4 collective-permute-start.16
  34.6 2.5 relay_in.2
  37.1 1.4 collective-permute-start
  40.5 16.4 %collective-permute-done.16.refs_9_ = bf16[256,512]{1,0:T(8,128)(2,1)} collective-permute-done((bf16[256,512]{1,0:T(8,128)(2,1)}, bf16[256,512]{1,0:T(8,128)(2,1)}, u32[]{:S(2)}, u32[]{:S(2)}) %collective-permute-start.16) | collective-permute-done | bytes 262176 | tf_op jit(solution)/shard_map/ppermute | solution.py:638
  57.8 1.7 collective-permute-start.19
  60.4 11.0 %collective-permute-done.18.refs_11_ = bf16[256,512]{1,0:T(8,128)(2,1)S(1)} collective-permute-done((bf16[256,512]{1,0:T(8,128)(2,1)}, bf16[256,512]{1,0:T(8,128)(2,1)S(1)}, u32[]{:S(2)}, u32[]{:S(2)}) %collective-permute-start.18) | collective-permute-done | bytes 262176 | tf_op jit(solution)/shard_map/ppermute | solution.py:638
  71.4 13.9 %collective-permute-done.2.refs_4_ = bf16[2,128,1024]{2,1,0:T(8,128)(2,1)S(1)} collective-permute-done((bf16[2,128,1024]{2,1,0:T(8,128)(2,1)}, bf16[2,128,1024]{2,1,0:T(8,128)(2,1)S(1)}, u32[]{:S(2)}, u32[]{:S(2)}) %collective-permute-start.2) | collective-permute-done | bytes 524320 | tf_op jit(solution)/shard_map/ppermute | solution.py:610
  86.1 13.2 %attend_first.1 = (bf16[8,256,512]{2,1,0:T(8,128)(2,1)}, bf16[2,128,512]{2,1,0:T(8,128)(2,1)}, bf16[2,128,512]{2,1,0:T(8,128)(2,1)}, bf16[2,128,512]{2,1,0:T(8,1...) custom-call(s32[34]{0:T(128)} %concatenate.7.refs_0_, bf16[2,128,1024]{2,1,0:T(8,128)(2,1)} %get-tuple-element.46.refs_1_, ...), custom_call_target="tpu_custom_call" | custom-call | flops 2684354560 | bytes 12582912 | tf_op jit(solution)/shard_map/attend_first/pallas_call | solution.py:414
  99.4 6.0 %all-to-all-start.3 = ((bf16[8,256,512]{2,1,0:T(8,128)(2,1)}), bf16[8,256,512]{2,1,0:T(8,128)(2,1)}, u32[]{:S(2)}, u32[]{:S(2)}) async-start(bf16[8,256,512]{2,1,0:T(8,128)(2,1)} %get-tuple-element.87), calls=%async_computation.3 | async-start | bytes 4194304 | tf_op jit(solution)/shard_map/all_to_all | solution.py:607
  105.4 2.5 pack_grad.2
  107.9 1.4 collective-permute-start.6
  110.0 1.4 collective-permute-start.9
  112.5 2.0 relay_in.3
  114.5 21.2 %collective-permute-done.6.refs_10_ = bf16[256,512]{1,0:T(8,128)(2,1)S(1)} collective-permute-done((bf16[256,512]{1,0:T(8,128)(2,1)}, bf16[256,512]{1,0:T(8,128)(2,1)S(1)}, u32[]{:S(2)}, u32[]{:S(2)}) %collective-permute-start.6) | collective-permute-done | bytes 262176 | tf_op jit(solution)/shard_map/ppermute | solution.py:638
  135.8 2.6 collective-permute-start.11
  138.4 4.0 %collective-permute-done.8.refs_12_ = bf16[256,512]{1,0:T(8,128)(2,1)S(1)} collective-permute-done((bf16[256,512]{1,0:T(8,128)(2,1)}, bf16[256,512]{1,0:T(8,128)(2,1)S(1)}, u32[]{:S(2)}, u32[]{:S(2)}) %collective-permute-start.8) | collective-permute-done | bytes 262176 | tf_op jit(solution)/shard_map/ppermute | solution.py:638
  142.5 3.1 %collective-permute-start.4 = (bf16[2,128,512]{2,1,0:T(8,128)(2,1)}, bf16[2,128,512]{2,1,0:T(8,128)(2,1)S(1)}, u32[]{:S(2)}, u32[]{:S(2)}) collective-permute-start(bf16[2,128,512]{2,1,0:T(8,128)(2,1)} %get-tuple-element.52), channel_id=1, source_target_pairs={{0,4},{1,5},{2,6},{3,7},{4,0},{5,1},{6,2},{7,3},{8,12},{9,13},{10,... | collective-permute-start | bytes 786440 | tf_op jit(solution)/shard_map/ppermute | solution.py:610
  145.6 2.4 collective-permute-done.10.refs_14_
  148.1 2.0 collective-permute-start.5
  150.0 6.9 %collective-permute-done.11.refs_15_ = bf16[256,512]{1,0:T(8,128)(2,1)S(1)} collective-permute-done((bf16[256,512]{1,0:T(8,128)(2,1)}, bf16[256,512]{1,0:T(8,128)(2,1)S(1)}, u32[]{:S(2)}, u32[]{:S(2)}) %collective-permute-start.11) | collective-permute-done | bytes 262176 | tf_op jit(solution)/shard_map/ppermute | solution.py:638
  157.1 3.1 %collective-permute-start.30 = (bf16[2,128,512]{2,1,0:T(8,128)(2,1)S(1)}, bf16[2,128,512]{2,1,0:T(8,128)(2,1)S(1)}, u32[]{:S(2)}, u32[]{:S(2)}) collective-permute-start(bf16[2,128,512]{2,1,0:T(8,128)(2,1)S(1)} %copy-done.19), channel_id=1, source_target_pairs={{0,4},{1,5},{2,6},{3,7},{4,0},{5,1},{6,2},{7,3},{8,12},{9,13},{10,... | collective-permute-start | bytes 786440 | tf_op jit(solution)/shard_map/ppermute | solution.py:610
  160.3 3.1 %collective-permute-done.4.refs_7_ = bf16[2,128,512]{2,1,0:T(8,128)(2,1)S(1)} collective-permute-done((bf16[2,128,512]{2,1,0:T(8,128)(2,1)}, bf16[2,128,512]{2,1,0:T(8,128)(2,1)S(1)}, u32[]{:S(2)}, u32[]{:S(2)}) %collective-permute-start.4) | collective-permute-done | bytes 262176 | tf_op jit(solution)/shard_map/ppermute | solution.py:610
  163.4 16.8 %collective-permute-done.5.refs_8_ = bf16[2,128,512]{2,1,0:T(8,128)(2,1)S(1)} collective-permute-done((bf16[2,128,512]{2,1,0:T(8,128)(2,1)}, bf16[2,128,512]{2,1,0:T(8,128)(2,1)S(1)}, u32[]{:S(2)}, u32[]{:S(2)}) %collective-permute-start.5) | collective-permute-done | bytes 262176 | tf_op jit(solution)/shard_map/ppermute | solution.py:610
  181.0 13.8 %attend_last.1 = (bf16[8,384,512]{2,1,0:T(8,128)(2,1)}, bf16[8,128,512]{2,1,0:T(8,128)(2,1)}, f32[8,128,256]{2,1,0:T(8,128)}, bf16[6,128,256]{2,1,0:T(8,128)(2,1)}) custom-call(s32[34]{0:T(128)} %concatenate.7.refs_0_, bf16[2,128,1024]{2,1,0:T(8,128)(2,1)} %get-tuple-element.46.refs_1_, bf16[2,128,1024]{2,1,0:T(8,128)(2,1)} %copy-done.14, ...), custom_call_target="tpu_custom_call" | custom-call | flops 2684354560 | bytes 12582912 | tf_op jit(solution)/shard_map/attend_last/pallas_call | solution.py:414
  195.6 2.0 relay_out.1
  197.7 4.9 %all-to-all-start.2 = ((bf16[8,384,512]{2,1,0:T(8,128)(2,1)}), bf16[8,384,512]{2,1,0:T(8,128)(2,1)}, u32[]{:S(2)}, u32[]{:S(2)}) async-start(bf16[8,384,512]{2,1,0:T(8,128)(2,1)} %relay_out.1), calls=%async_computation.2 | async-start | bytes 6291456 | tf_op jit(solution)/shard_map/all_to_all | solution.py:607
  202.6 6.0 %collective-permute-start.20 = (bf16[6,128,256]{2,1,0:T(8,128)(2,1)S(1)}, bf16[6,128,256]{2,1,0:T(8,128)(2,1)S(1)}, u32[]{:S(2)}, u32[]{:S(2)}) collective-permute-start(bf16[6,128,256]{2,1,0:T(8,128)(2,1)S(1)} %copy-done.17), channel_id=1, source_target_pairs={{2,0},{3,1},{4,2},{5,3},{6,4},{7,5},{10,8},{11,9},{12,10},{13,11},... | collective-permute-start | bytes 1179656 | tf_op jit(solution)/shard_map/ppermute | solution.py:672
  208.6 8.3 %collective-permute-done.20.back_ref = bf16[6,128,256]{2,1,0:T(8,128)(2,1)S(1)} collective-permute-done((bf16[6,128,256]{2,1,0:T(8,128)(2,1)S(1)}, bf16[6,128,256]{2,1,0:T(8,128)(2,1)S(1)}, u32[]{:S(2)}, u32[]{:S(2)}) %collective-permute-start.20) | collective-permute-done | bytes 393248 | tf_op jit(solution)/shard_map/ppermute | solution.py:672
  217.7 2.9 %finish.1 = (bf16[128,768]{1,0:T(8,128)(2,1)}, bf16[128,768]{1,0:T(8,128)(2,1)}, bf16[128,768]{1,0:T(8,128)(2,1)}, bf16[128,768]{1,0:T(8,128)(2,1)}, bf16[128,76...) custom-call(s32[1]{0:T(128)} %bitcast.1.core_ref, ...), custom_call_target="tpu_custom_call" | custom-call | bytes 5242880 | tf_op jit(solution)/shard_map/finish/pallas_call | solution.py:460
  220.6 6.1 %collective-permute-start.21 = (bf16[128,768]{1,0:T(8,128)(2,1)}, bf16[128,768]{1,0:T(8,128)(2,1)S(1)}, u32[]{:S(2)}, u32[]{:S(2)}) collective-permute-start(bf16[128,768]{1,0:T(8,128)(2,1)} %get-tuple-element.74), channel_id=1, source_target_pairs={{0,0},{1,1},{2,8},{3,9},{4,16},{5,17},{6,24},{7,25},{8,2},{9,3},{1... | collective-permute-start | bytes 589832 | tf_op jit(solution)/shard_map/ppermute | solution.py:617
  227.6 3.5 %collective-permute-start.23 = (bf16[128,768]{1,0:T(8,128)(2,1)}, bf16[128,768]{1,0:T(8,128)(2,1)S(1)}, u32[]{:S(2)}, u32[]{:S(2)}) collective-permute-start(bf16[128,768]{1,0:T(8,128)(2,1)} %get-tuple-element.76), channel_id=1, source_target_pairs={{0,2},{1,3},{2,10},{3,11},{4,18},{5,19},{6,26},{7,27},{8,0},{9,1},... | collective-permute-start | bytes 589832 | tf_op jit(solution)/shard_map/ppermute | solution.py:617
  231.4 17.0 %collective-permute-done.21.refs_1_ = bf16[128,768]{1,0:T(8,128)(2,1)S(1)} collective-permute-done((bf16[128,768]{1,0:T(8,128)(2,1)}, bf16[128,768]{1,0:T(8,128)(2,1)S(1)}, u32[]{:S(2)}, u32[]{:S(2)}) %collective-permute-start.21) | collective-permute-done | bytes 196640 | tf_op jit(solution)/shard_map/ppermute | solution.py:617
  248.4 5.0 %collective-permute-done.22.refs_2_ = bf16[128,768]{1,0:T(8,128)(2,1)S(1)} collective-permute-done((bf16[128,768]{1,0:T(8,128)(2,1)}, bf16[128,768]{1,0:T(8,128)(2,1)S(1)}, u32[]{:S(2)}, u32[]{:S(2)}) %collective-permute-start.22) | collective-permute-done | bytes 196640 | tf_op jit(solution)/shard_map/ppermute | solution.py:617
  253.4 1.9 collective-permute-start.27
  255.4 1.5 collective-permute-done.23.refs_3_
  257.3 2.4 place_out.1.refs_10_
  259.8 2.1 collective-permute-done.24.refs_4_
  261.9 6.2 %collective-permute-done.26.refs_6_ = bf16[128,768]{1,0:T(8,128)(2,1)S(1)} collective-permute-done((bf16[128,768]{1,0:T(8,128)(2,1)}, bf16[128,768]{1,0:T(8,128)(2,1)S(1)}, u32[]{:S(2)}, u32[]{:S(2)}) %collective-permute-start.26) | collective-permute-done | bytes 196640 | tf_op jit(solution)/shard_map/ppermute | solution.py:617
  268.1 3.6 %collective-permute-done.27.refs_7_ = bf16[128,768]{1,0:T(8,128)(2,1)S(1)} collective-permute-done((bf16[128,768]{1,0:T(8,128)(2,1)}, bf16[128,768]{1,0:T(8,128)(2,1)S(1)}, u32[]{:S(2)}, u32[]{:S(2)}) %collective-permute-start.27) | collective-permute-done | bytes 196640 | tf_op jit(solution)/shard_map/ppermute | solution.py:617
  271.7 4.7 %collective-permute-done.28.refs_8_ = bf16[128,768]{1,0:T(8,128)(2,1)S(1)} collective-permute-done((bf16[128,768]{1,0:T(8,128)(2,1)}, bf16[128,768]{1,0:T(8,128)(2,1)S(1)}, u32[]{:S(2)}, u32[]{:S(2)}) %collective-permute-start.28) | collective-permute-done | bytes 196640 | tf_op jit(solution)/shard_map/ppermute | solution.py:617
  277.1 4.4 %place_last.1 = (bf16[256,8192]{1,0:T(8,128)(2,1)}, bf16[128,8192]{1,0:T(8,128)(2,1)}, bf16[128,1024]{1,0:T(8,128)(2,1)}, bf16[128,1024]{1,0:T(8,128)(2,1)}) custom-call(s32[1]{0:T(128)} %bitcast.refs_0_, bf16[128,768]{1,0:T(8,128)(2,1)} %copy-done.6, bf16[128,768]{1,0:T(8,128)(2,1)} %copy-done.7, ...), custom_call_target="tpu_custom_call", output_to_operand_aliasing={{0}: (10, {})} | custom-call | bytes 10485760 | tf_op jit(solution)/shard_map/place_last/pallas_call | solution.py:529
  (110 shorter events, 13.3 us)
Async XLA Ops:
  0.6 39.6 %copy-start = (s32[4,4,4]{2,1,0:T(4,128)S(1)}, s32[4,4,4]{2,1,0:T(4,128)}, u32[]{:S(2)}) copy-start(s32[4,4,4]{2,1,0:T(4,128)} %param.11) | copy-start | bytes 772
  3.1 24.4 %all-to-all-start = ((bf16[8,128,768]{2,1,0:T(8,128)(2,1)}), bf16[8,128,768]{2,1,0:T(8,128)(2,1)S(1)}, u32[]{:S(2)}, u32[]{:S(2)}) async-start(bf16[8,128,768]{2,1,0:T(8,128)(2,1)} %shard_map.93), calls=%async_computation | async-start | bytes 3145728 | tf_op jit(solution)/shard_map/all_to_all | solution.py:607
  9.9 27.1 %collective-permute-start.13 = (bf16[256,512]{1,0:T(8,128)(2,1)}, bf16[256,512]{1,0:T(8,128)(2,1)S(1)}, u32[]{:S(2)}, u32[]{:S(2)}) collective-permute-start(bf16[256,512]{1,0:T(8,128)(2,1)} %get-tuple-element.63), channel_id=1, source_target_pairs={{0,1},{1,0},{2,3},{3,2},{4,5},{5,4},{6,7},{7,6},{8,9},{9,8},{10,11... | collective-permute-start | bytes 786440 | tf_op jit(solution)/shard_map/ppermute | solution.py:638
  11.3 27.1 %collective-permute-start.14 = (bf16[256,512]{1,0:T(8,128)(2,1)}, bf16[256,512]{1,0:T(8,128)(2,1)}, u32[]{:S(2)}, u32[]{:S(2)}) collective-permute-start(bf16[256,512]{1,0:T(8,128)(2,1)} %get-tuple-element.64), channel_id=1, source_target_pairs={{0,8},{1,9},{2,10},{3,11},{4,12},{5,13},{6,14},{7,15},{8,0},{9,1},... | collective-permute-start | bytes 786440 | tf_op jit(solution)/shard_map/ppermute | solution.py:638
  12.0 27.1 %collective-permute-start.15 = (bf16[256,512]{1,0:T(8,128)(2,1)}, bf16[256,512]{1,0:T(8,128)(2,1)}, u32[]{:S(2)}, u32[]{:S(2)}) collective-permute-start(bf16[256,512]{1,0:T(8,128)(2,1)} %get-tuple-element.65), channel_id=1, source_target_pairs={{0,9},{1,8},{2,11},{3,10},{4,13},{5,12},{6,15},{7,14},{8,1},{9,0},... | collective-permute-start | bytes 786440 | tf_op jit(solution)/shard_map/ppermute | solution.py:638
  14.1 45.4 %copy-start.33 = (s32[32]{0:T(128)S(1)}, s32[32]{0:T(128)}, u32[]{:S(2)}) copy-start(s32[32]{0:T(128)} %param.10) | copy-start | bytes 388
  27.5 71.8 %all-to-all-start.1 = ((bf16[8,128,512]{2,1,0:T(8,128)(2,1)}), bf16[8,128,512]{2,1,0:T(8,128)(2,1)}, u32[]{:S(2)}, u32[]{:S(2)}) async-start(bf16[8,128,512]{2,1,0:T(8,128)(2,1)} %shard_map.94), calls=%async_computation.1 | async-start | bytes 2097152 | tf_op jit(solution)/shard_map/all_to_all | solution.py:607
  32.0 24.8 %collective-permute-start.16 = (bf16[256,512]{1,0:T(8,128)(2,1)}, bf16[256,512]{1,0:T(8,128)(2,1)}, u32[]{:S(2)}, u32[]{:S(2)}) collective-permute-start(bf16[256,512]{1,0:T(8,128)(2,1)} %get-tuple-element.66), channel_id=1, source_target_pairs={{0,16},{1,17},{2,18},{3,19},{4,20},{5,21},{6,22},{7,23},{8,24},{9,... | collective-permute-start | bytes 786440 | tf_op jit(solution)/shard_map/ppermute | solution.py:638
  33.4 24.4 %collective-permute-start.17 = (bf16[256,512]{1,0:T(8,128)(2,1)}, bf16[256,512]{1,0:T(8,128)(2,1)}, u32[]{:S(2)}, u32[]{:S(2)}) collective-permute-start(bf16[256,512]{1,0:T(8,128)(2,1)} %get-tuple-element.67), channel_id=1, source_target_pairs={{0,17},{1,16},{2,19},{3,18},{4,21},{5,20},{6,23},{7,22},{8,25},{9,... | collective-permute-start | bytes 786440 | tf_op jit(solution)/shard_map/ppermute | solution.py:638
  37.1 34.3 %collective-permute-start = (bf16[2,128,1024]{2,1,0:T(8,128)(2,1)}, bf16[2,128,1024]{2,1,0:T(8,128)(2,1)S(1)}, u32[]{:S(2)}, u32[]{:S(2)}) collective-permute-start(bf16[2,128,1024]{2,1,0:T(8,128)(2,1)} %get-tuple-element.47), channel_id=1, source_target_pairs={{0,2},{1,3},{2,0},{3,1},{4,6},{5,7},{6,4},{7,5},{8,10},{9,11},{10,... | collective-permute-start | bytes 1572872 | tf_op jit(solution)/shard_map/ppermute | solution.py:610
  38.4 32.9 %collective-permute-start.1 = (bf16[2,128,1024]{2,1,0:T(8,128)(2,1)}, bf16[2,128,1024]{2,1,0:T(8,128)(2,1)S(1)}, u32[]{:S(2)}, u32[]{:S(2)}) collective-permute-start(bf16[2,128,1024]{2,1,0:T(8,128)(2,1)} %get-tuple-element.48), channel_id=1, source_target_pairs={{0,4},{1,5},{2,6},{3,7},{4,0},{5,1},{6,2},{7,3},{8,12},{9,13},{10,... | collective-permute-start | bytes 1572872 | tf_op jit(solution)/shard_map/ppermute | solution.py:610
  39.1 46.2 %collective-permute-start.2 = (bf16[2,128,1024]{2,1,0:T(8,128)(2,1)}, bf16[2,128,1024]{2,1,0:T(8,128)(2,1)S(1)}, u32[]{:S(2)}, u32[]{:S(2)}) collective-permute-start(bf16[2,128,1024]{2,1,0:T(8,128)(2,1)} %get-tuple-element.49), channel_id=1, source_target_pairs={{0,6},{1,7},{2,4},{3,5},{4,2},{5,3},{6,0},{7,1},{8,14},{9,15},{10,... | collective-permute-start | bytes 1572872 | tf_op jit(solution)/shard_map/ppermute | solution.py:610
  56.9 14.5 %collective-permute-start.18 = (bf16[256,512]{1,0:T(8,128)(2,1)}, bf16[256,512]{1,0:T(8,128)(2,1)S(1)}, u32[]{:S(2)}, u32[]{:S(2)}) collective-permute-start(bf16[256,512]{1,0:T(8,128)(2,1)} %get-tuple-element.68), channel_id=1, source_target_pairs={{0,24},{1,25},{2,26},{3,27},{4,28},{5,29},{6,30},{7,31},{8,16},{9,... | collective-permute-start | bytes 786440 | tf_op jit(solution)/shard_map/ppermute | solution.py:638
  57.8 13.5 %collective-permute-start.19 = (bf16[256,512]{1,0:T(8,128)(2,1)}, bf16[256,512]{1,0:T(8,128)(2,1)S(1)}, u32[]{:S(2)}, u32[]{:S(2)}) collective-permute-start(bf16[256,512]{1,0:T(8,128)(2,1)} %get-tuple-element.69), channel_id=1, source_target_pairs={{0,25},{1,24},{2,27},{3,26},{4,29},{5,28},{6,31},{7,30},{8,17},{9,... | collective-permute-start | bytes 786440 | tf_op jit(solution)/shard_map/ppermute | solution.py:638
  99.4 98.3 %all-to-all-start.3 = ((bf16[8,256,512]{2,1,0:T(8,128)(2,1)}), bf16[8,256,512]{2,1,0:T(8,128)(2,1)}, u32[]{:S(2)}, u32[]{:S(2)}) async-start(bf16[8,256,512]{2,1,0:T(8,128)(2,1)} %get-tuple-element.87), calls=%async_computation.3 | async-start | bytes 4194304 | tf_op jit(solution)/shard_map/all_to_all | solution.py:607
  105.4 51.6 %copy-start.20 = (bf16[2,128,512]{2,1,0:T(8,128)(2,1)S(1)}, bf16[2,128,512]{2,1,0:T(8,128)(2,1)}, u32[]{:S(2)}) copy-start(bf16[2,128,512]{2,1,0:T(8,128)(2,1)} %get-tuple-element.83) | copy-start | bytes 786436
  105.4 51.7 %copy-start.19 = (bf16[2,128,512]{2,1,0:T(8,128)(2,1)S(1)}, bf16[2,128,512]{2,1,0:T(8,128)(2,1)}, u32[]{:S(2)}) copy-start(bf16[2,128,512]{2,1,0:T(8,128)(2,1)} %get-tuple-element.84) | copy-start | bytes 786436
  105.4 54.8 %copy-start.18 = (bf16[2,128,512]{2,1,0:T(8,128)(2,1)S(1)}, bf16[2,128,512]{2,1,0:T(8,128)(2,1)}, u32[]{:S(2)}) copy-start(bf16[2,128,512]{2,1,0:T(8,128)(2,1)} %get-tuple-element.85) | copy-start | bytes 786436
  107.9 27.9 %collective-permute-start.6 = (bf16[256,512]{1,0:T(8,128)(2,1)}, bf16[256,512]{1,0:T(8,128)(2,1)S(1)}, u32[]{:S(2)}, u32[]{:S(2)}) collective-permute-start(bf16[256,512]{1,0:T(8,128)(2,1)} %get-tuple-element.55), channel_id=1, source_target_pairs={{0,1},{1,0},{2,3},{3,2},{4,5},{5,4},{6,7},{7,6},{8,9},{9,8},{10,11... | collective-permute-start | bytes 786440 | tf_op jit(solution)/shard_map/ppermute | solution.py:638
  109.3 29.1 %collective-permute-start.7 = (bf16[256,512]{1,0:T(8,128)(2,1)}, bf16[256,512]{1,0:T(8,128)(2,1)S(1)}, u32[]{:S(2)}, u32[]{:S(2)}) collective-permute-start(bf16[256,512]{1,0:T(8,128)(2,1)} %get-tuple-element.56), channel_id=1, source_target_pairs={{0,8},{1,9},{2,10},{3,11},{4,12},{5,13},{6,14},{7,15},{8,0},{9,1},... | collective-permute-start | bytes 786440 | tf_op jit(solution)/shard_map/ppermute | solution.py:638
  110.0 32.5 %collective-permute-start.8 = (bf16[256,512]{1,0:T(8,128)(2,1)}, bf16[256,512]{1,0:T(8,128)(2,1)S(1)}, u32[]{:S(2)}, u32[]{:S(2)}) collective-permute-start(bf16[256,512]{1,0:T(8,128)(2,1)} %get-tuple-element.57), channel_id=1, source_target_pairs={{0,9},{1,8},{2,11},{3,10},{4,13},{5,12},{6,15},{7,14},{8,1},{9,0},... | collective-permute-start | bytes 786440 | tf_op jit(solution)/shard_map/ppermute | solution.py:638
  110.0 32.5 %collective-permute-start.9 = (bf16[256,512]{1,0:T(8,128)(2,1)}, bf16[256,512]{1,0:T(8,128)(2,1)S(1)}, u32[]{:S(2)}, u32[]{:S(2)}) collective-permute-start(bf16[256,512]{1,0:T(8,128)(2,1)} %get-tuple-element.58), channel_id=1, source_target_pairs={{0,16},{1,17},{2,18},{3,19},{4,20},{5,21},{6,22},{7,23},{8,24},{9,... | collective-permute-start | bytes 786440 | tf_op jit(solution)/shard_map/ppermute | solution.py:638
  111.3 36.7 %collective-permute-start.10 = (bf16[256,512]{1,0:T(8,128)(2,1)}, bf16[256,512]{1,0:T(8,128)(2,1)}, u32[]{:S(2)}, u32[]{:S(2)}) collective-permute-start(bf16[256,512]{1,0:T(8,128)(2,1)} %get-tuple-element.59), channel_id=1, source_target_pairs={{0,17},{1,16},{2,19},{3,18},{4,21},{5,20},{6,23},{7,22},{8,25},{9,... | collective-permute-start | bytes 786440 | tf_op jit(solution)/shard_map/ppermute | solution.py:638
  135.8 45.2 %copy-start.22 = (bf16[256,512]{1,0:T(8,128)(2,1)}, bf16[256,512]{1,0:T(8,128)(2,1)S(1)}, u32[]{:S(2)}) copy-start(bf16[256,512]{1,0:T(8,128)(2,1)S(1)} %collective-permute-done.6.refs_10_) | copy-start | bytes 786436
  135.8 21.2 %collective-permute-start.11 = (bf16[256,512]{1,0:T(8,128)(2,1)}, bf16[256,512]{1,0:T(8,128)(2,1)S(1)}, u32[]{:S(2)}, u32[]{:S(2)}) collective-permute-start(bf16[256,512]{1,0:T(8,128)(2,1)} %get-tuple-element.60), channel_id=1, source_target_pairs={{0,24},{1,25},{2,26},{3,27},{4,28},{5,29},{6,30},{7,31},{8,16},{9,... | collective-permute-start | bytes 786440 | tf_op jit(solution)/shard_map/ppermute | solution.py:638
  138.4 18.6 %copy-start.23 = (bf16[256,512]{1,0:T(8,128)(2,1)}, bf16[256,512]{1,0:T(8,128)(2,1)S(1)}, u32[]{:S(2)}) copy-start(bf16[256,512]{1,0:T(8,128)(2,1)S(1)} %collective-permute-done.7.refs_11_) | copy-start | bytes 786436
  138.4 18.6 %collective-permute-start.12 = (bf16[256,512]{1,0:T(8,128)(2,1)}, bf16[256,512]{1,0:T(8,128)(2,1)S(1)}, u32[]{:S(2)}, u32[]{:S(2)}) collective-permute-start(bf16[256,512]{1,0:T(8,128)(2,1)} %get-tuple-element.61), channel_id=1, source_target_pairs={{0,25},{1,24},{2,27},{3,26},{4,29},{5,28},{6,31},{7,30},{8,17},{9,... | collective-permute-start | bytes 786440 | tf_op jit(solution)/shard_map/ppermute | solution.py:638
  142.5 14.5 %copy-start.24 = (bf16[256,512]{1,0:T(8,128)(2,1)}, bf16[256,512]{1,0:T(8,128)(2,1)S(1)}, u32[]{:S(2)}) copy-start(bf16[256,512]{1,0:T(8,128)(2,1)S(1)} %collective-permute-done.8.refs_12_) | copy-start | bytes 786436
  142.5 17.7 %collective-permute-start.3 = (bf16[2,128,512]{2,1,0:T(8,128)(2,1)}, bf16[2,128,512]{2,1,0:T(8,128)(2,1)S(1)}, u32[]{:S(2)}, u32[]{:S(2)}) collective-permute-start(bf16[2,128,512]{2,1,0:T(8,128)(2,1)} %get-tuple-element.51), channel_id=1, source_target_pairs={{0,2},{1,3},{2,0},{3,1},{4,6},{5,7},{6,4},{7,5},{8,10},{9,11},{10,... | collective-permute-start | bytes 786440 | tf_op jit(solution)/shard_map/ppermute | solution.py:610
  142.5 17.7 %copy-start.25 = (bf16[256,512]{1,0:T(8,128)(2,1)}, bf16[256,512]{1,0:T(8,128)(2,1)S(1)}, u32[]{:S(2)}) copy-start(bf16[256,512]{1,0:T(8,128)(2,1)S(1)} %collective-permute-done.9.refs_13_) | copy-start | bytes 786436
  142.5 20.9 %collective-permute-start.4 = (bf16[2,128,512]{2,1,0:T(8,128)(2,1)}, bf16[2,128,512]{2,1,0:T(8,128)(2,1)S(1)}, u32[]{:S(2)}, u32[]{:S(2)}) collective-permute-start(bf16[2,128,512]{2,1,0:T(8,128)(2,1)} %get-tuple-element.52), channel_id=1, source_target_pairs={{0,4},{1,5},{2,6},{3,7},{4,0},{5,1},{6,2},{7,3},{8,12},{9,13},{10,... | collective-permute-start | bytes 786440 | tf_op jit(solution)/shard_map/ppermute | solution.py:610
  148.1 32.2 %collective-permute-start.5 = (bf16[2,128,512]{2,1,0:T(8,128)(2,1)}, bf16[2,128,512]{2,1,0:T(8,128)(2,1)S(1)}, u32[]{:S(2)}, u32[]{:S(2)}) collective-permute-start(bf16[2,128,512]{2,1,0:T(8,128)(2,1)} %get-tuple-element.53), channel_id=1, source_target_pairs={{0,6},{1,7},{2,4},{3,5},{4,2},{5,3},{6,0},{7,1},{8,14},{9,15},{10,... | collective-permute-start | bytes 786440 | tf_op jit(solution)/shard_map/ppermute | solution.py:610
  156.9 37.8 %collective-permute-start.29 = (bf16[2,128,512]{2,1,0:T(8,128)(2,1)S(1)}, bf16[2,128,512]{2,1,0:T(8,128)(2,1)S(1)}, u32[]{:S(2)}, u32[]{:S(2)}) collective-permute-start(bf16[2,128,512]{2,1,0:T(8,128)(2,1)S(1)} %copy-done.20), channel_id=1, source_target_pairs={{0,2},{1,3},{2,0},{3,1},{4,6},{5,7},{6,4},{7,5},{8,10},{9,11},{10,... | collective-permute-start | bytes 786440 | tf_op jit(solution)/shard_map/ppermute | solution.py:610
  157.1 37.7 %collective-permute-start.30 = (bf16[2,128,512]{2,1,0:T(8,128)(2,1)S(1)}, bf16[2,128,512]{2,1,0:T(8,128)(2,1)S(1)}, u32[]{:S(2)}, u32[]{:S(2)}) collective-permute-start(bf16[2,128,512]{2,1,0:T(8,128)(2,1)S(1)} %copy-done.19), channel_id=1, source_target_pairs={{0,4},{1,5},{2,6},{3,7},{4,0},{5,1},{6,2},{7,3},{8,12},{9,13},{10,... | collective-permute-start | bytes 786440 | tf_op jit(solution)/shard_map/ppermute | solution.py:610
  160.2 20.1 %copy-start.28 = (bf16[2,128,512]{2,1,0:T(8,128)(2,1)}, bf16[2,128,512]{2,1,0:T(8,128)(2,1)S(1)}, u32[]{:S(2)}) copy-start(bf16[2,128,512]{2,1,0:T(8,128)(2,1)S(1)} %collective-permute-done.3.refs_6_) | copy-start | bytes 786436
  160.2 34.6 %collective-permute-start.31 = (bf16[2,128,512]{2,1,0:T(8,128)(2,1)S(1)}, bf16[2,128,512]{2,1,0:T(8,128)(2,1)S(1)}, u32[]{:S(2)}, u32[]{:S(2)}) collective-permute-start(bf16[2,128,512]{2,1,0:T(8,128)(2,1)S(1)} %copy-done.18), channel_id=1, source_target_pairs={{0,6},{1,7},{2,4},{3,5},{4,2},{5,3},{6,0},{7,1},{8,14},{9,15},{10,... | collective-permute-start | bytes 786440 | tf_op jit(solution)/shard_map/ppermute | solution.py:610
  163.4 16.9 %copy-start.29 = (bf16[2,128,512]{2,1,0:T(8,128)(2,1)}, bf16[2,128,512]{2,1,0:T(8,128)(2,1)S(1)}, u32[]{:S(2)}) copy-start(bf16[2,128,512]{2,1,0:T(8,128)(2,1)S(1)} %collective-permute-done.4.refs_7_) | copy-start | bytes 786436
  197.7 78.8 %all-to-all-start.2 = ((bf16[8,384,512]{2,1,0:T(8,128)(2,1)}), bf16[8,384,512]{2,1,0:T(8,128)(2,1)}, u32[]{:S(2)}, u32[]{:S(2)}) async-start(bf16[8,384,512]{2,1,0:T(8,128)(2,1)} %relay_out.1), calls=%async_computation.2 | async-start | bytes 6291456 | tf_op jit(solution)/shard_map/all_to_all | solution.py:607
  202.6 14.3 %collective-permute-start.20 = (bf16[6,128,256]{2,1,0:T(8,128)(2,1)S(1)}, bf16[6,128,256]{2,1,0:T(8,128)(2,1)S(1)}, u32[]{:S(2)}, u32[]{:S(2)}) collective-permute-start(bf16[6,128,256]{2,1,0:T(8,128)(2,1)S(1)} %copy-done.17), channel_id=1, source_target_pairs={{2,0},{3,1},{4,2},{5,3},{6,4},{7,5},{10,8},{11,9},{12,10},{13,11},... | collective-permute-start | bytes 1179656 | tf_op jit(solution)/shard_map/ppermute | solution.py:672
  220.6 27.8 %collective-permute-start.21 = (bf16[128,768]{1,0:T(8,128)(2,1)}, bf16[128,768]{1,0:T(8,128)(2,1)S(1)}, u32[]{:S(2)}, u32[]{:S(2)}) collective-permute-start(bf16[128,768]{1,0:T(8,128)(2,1)} %get-tuple-element.74), channel_id=1, source_target_pairs={{0,0},{1,1},{2,8},{3,9},{4,16},{5,17},{6,24},{7,25},{8,2},{9,3},{1... | collective-permute-start | bytes 589832 | tf_op jit(solution)/shard_map/ppermute | solution.py:617
  226.7 26.8 %collective-permute-start.22 = (bf16[128,768]{1,0:T(8,128)(2,1)}, bf16[128,768]{1,0:T(8,128)(2,1)S(1)}, u32[]{:S(2)}, u32[]{:S(2)}) collective-permute-start(bf16[128,768]{1,0:T(8,128)(2,1)} %get-tuple-element.75), channel_id=1, source_target_pairs={{0,1},{1,0},{2,9},{3,8},{4,17},{5,16},{6,25},{7,24},{8,3},{9,2},{1... | collective-permute-start | bytes 589832 | tf_op jit(solution)/shard_map/ppermute | solution.py:617
  227.6 29.2 %collective-permute-start.23 = (bf16[128,768]{1,0:T(8,128)(2,1)}, bf16[128,768]{1,0:T(8,128)(2,1)S(1)}, u32[]{:S(2)}, u32[]{:S(2)}) collective-permute-start(bf16[128,768]{1,0:T(8,128)(2,1)} %get-tuple-element.76), channel_id=1, source_target_pairs={{0,2},{1,3},{2,10},{3,11},{4,18},{5,19},{6,26},{7,27},{8,0},{9,1},... | collective-permute-start | bytes 589832 | tf_op jit(solution)/shard_map/ppermute | solution.py:617
  231.2 30.7 %collective-permute-start.24 = (bf16[128,768]{1,0:T(8,128)(2,1)}, bf16[128,768]{1,0:T(8,128)(2,1)S(1)}, u32[]{:S(2)}, u32[]{:S(2)}) collective-permute-start(bf16[128,768]{1,0:T(8,128)(2,1)} %get-tuple-element.77), channel_id=1, source_target_pairs={{0,3},{1,2},{2,11},{3,10},{4,19},{5,18},{6,27},{7,26},{8,1},{9,0},... | collective-permute-start | bytes 589832 | tf_op jit(solution)/shard_map/ppermute | solution.py:617
  231.4 30.5 %collective-permute-start.25 = (bf16[128,768]{1,0:T(8,128)(2,1)}, bf16[128,768]{1,0:T(8,128)(2,1)S(1)}, u32[]{:S(2)}, u32[]{:S(2)}) collective-permute-start(bf16[128,768]{1,0:T(8,128)(2,1)} %get-tuple-element.78), channel_id=1, source_target_pairs={{0,4},{1,5},{2,12},{3,13},{4,20},{5,21},{6,28},{7,29},{8,6},{9,7},... | collective-permute-start | bytes 589832 | tf_op jit(solution)/shard_map/ppermute | solution.py:617
  248.4 19.7 %collective-permute-start.26 = (bf16[128,768]{1,0:T(8,128)(2,1)}, bf16[128,768]{1,0:T(8,128)(2,1)S(1)}, u32[]{:S(2)}, u32[]{:S(2)}) collective-permute-start(bf16[128,768]{1,0:T(8,128)(2,1)} %get-tuple-element.79), channel_id=1, source_target_pairs={{0,5},{1,4},{2,13},{3,12},{4,21},{5,20},{6,29},{7,28},{8,7},{9,6},... | collective-permute-start | bytes 589832 | tf_op jit(solution)/shard_map/ppermute | solution.py:617
  253.4 18.3 %collective-permute-start.27 = (bf16[128,768]{1,0:T(8,128)(2,1)}, bf16[128,768]{1,0:T(8,128)(2,1)S(1)}, u32[]{:S(2)}, u32[]{:S(2)}) collective-permute-start(bf16[128,768]{1,0:T(8,128)(2,1)} %get-tuple-element.80), channel_id=1, source_target_pairs={{0,6},{1,7},{2,14},{3,15},{4,22},{5,23},{6,30},{7,31},{8,4},{9,5},... | collective-permute-start | bytes 589832 | tf_op jit(solution)/shard_map/ppermute | solution.py:617
  256.8 19.6 %collective-permute-start.28 = (bf16[128,768]{1,0:T(8,128)(2,1)}, bf16[128,768]{1,0:T(8,128)(2,1)S(1)}, u32[]{:S(2)}, u32[]{:S(2)}) collective-permute-start(bf16[128,768]{1,0:T(8,128)(2,1)} %get-tuple-element.81), channel_id=1, source_target_pairs={{0,7},{1,6},{2,15},{3,14},{4,23},{5,22},{6,31},{7,30},{8,5},{9,4},... | collective-permute-start | bytes 589832 | tf_op jit(solution)/shard_map/ppermute | solution.py:617
  261.9 14.5 %copy-start.9 = (bf16[128,768]{1,0:T(8,128)(2,1)}, bf16[128,768]{1,0:T(8,128)(2,1)S(1)}, u32[]{:S(2)}) copy-start(bf16[128,768]{1,0:T(8,128)(2,1)S(1)} %collective-permute-done.24.refs_4_) | copy-start | bytes 589828
  (22 other events, 132.4 us)
